TPU v7x, 128 devices: a whole 4x4x4 slice. The times are simulated.
128 devices in a mesh: orient: 32 (over x, z, y_lo), slab: 4 (over y_hi, core).
Axes of the slice: x: 4, y: 4 (y_hi: 2, y_lo: 2; y = y_hi * 2 + y_lo), z: 4, core: 2. Of those that a mesh axis runs over, the one named last changes fastest.
Arguments:
- volume: bfloat16 [32, 512, 8192], P('orient', 'slab'), may hold values from 0 to 2
- rays: bfloat16 [8192, 8, 128], replicated, may hold values from -0.0234375 to 0.0234375
- band_start: int32 [8, 32], P(None, 'orient'), may hold values from 0 to 63
- band_len: int32 [8, 32], P(None, 'orient'), may hold values from 32 to 64
- slot_image: int32 [32], replicated, may hold values from 0 to 31, each once
- measured: float32 [32, 512, 128], P('orient', 'slab'), may hold values from -6 to 6
- relax: float32 [32], P('orient'), may hold values from 0.25 to 1
Outputs:
- updated: bfloat16 [32, 512, 8192], P('orient', 'slab')
- residual: float32 [32, 512, 128], P('orient', 'slab')
Inputs may be any that keep to these rules, and one draw needn't show every extreme that they name: `slot_image`: every image number appears in exactly one slot. band_start + band_len stays below 128.
All inputs are finite; a program needn't handle non-finite values.
Results may differ from a plain program's by a relative error of at most 0.0055.
Values may be sent and summed in bfloat16 or wider, within the bound.
No kernel may reach another device: no remote copies, remote signals or barrier semaphores. Data moves between devices by JAX's collectives and lax.ppermute only.
A program may use at most 128 MiB of HBM per device.

v0:
```python
import math

import jax
import jax.numpy as jnp
from jax import lax
from jax.sharding import PartitionSpec as P

FRAMES = 4
SWEEPS = 2


huber_delta = 0.5
sweep_rate = 0.2


def extended_2(cells, sides, width):
    for axis, dim in sides:
        count = lax.axis_size(axis)
        ends = count - 1
        head = lax.slice_in_dim(cells, 0, width, axis=dim)
        tail = lax.slice_in_dim(cells, cells.shape[dim] - width, cells.shape[dim], axis=dim)
        cells = jnp.concatenate(
            [
                lax.ppermute(tail, axis, [(i, (i + 1) % count) for i in range(ends)]),
                cells,
                lax.ppermute(head, axis, [((i + 1) % count, i) for i in range(ends)]),
            ],
            axis=dim,
        )
    return cells


def smooth_pass(extended, first_row, total_rows):
    middle = extended[:, 1:-1]
    row_count = middle.shape[1]
    global_rows = first_row + 1 + jnp.arange(row_count, dtype=jnp.int32)
    has_above = (global_rows > 0)[None, :, None]
    has_below = (global_rows < total_rows - 1)[None, :, None]
    from_above = jnp.clip(middle - extended[:, :-2], -huber_delta, huber_delta)
    from_below = jnp.clip(middle - extended[:, 2:], -huber_delta, huber_delta)
    row_flux = jnp.where(has_above, from_above, 0.0) + jnp.where(has_below, from_below, 0.0)
    return middle - sweep_rate * row_flux


def local(volume, rays, band_start, band_len, slot_image, measured, relax):
    or_dev, row_dev, cell_count = volume.shape
    reflections_n, detector = (rays.shape[1], rays.shape[2])
    images_n = reflections_n * FRAMES
    orient_groups = lax.axis_size("orient")
    orients_all = or_dev * orient_groups
    orient_ids = lax.axis_index("orient") * or_dev + jnp.arange(or_dev, dtype=jnp.int32)
    reflections = jnp.arange(reflections_n, dtype=jnp.int32)
    frame_of = (orient_ids[:, None] + reflections[None, :]) % FRAMES
    frame_pick = (frame_of[:, :, None] == jnp.arange(FRAMES, dtype=jnp.int32)).astype(jnp.float32)
    columns = jnp.arange(detector, dtype=jnp.int32)
    inside = (columns >= band_start[:, :, None]) & (columns < (band_start + band_len)[:, :, None])
    band_mask = inside.astype(jnp.float32)
    inverse = (
        jnp.zeros((images_n,), jnp.int32).at[slot_image].set(jnp.arange(images_n, dtype=jnp.int32))
    )
    flat_rays = rays.reshape(cell_count, reflections_n * detector)
    projected = jnp.dot(
        volume.reshape(or_dev * row_dev, cell_count), flat_rays, preferred_element_type=jnp.float32
    )
    projected = projected.reshape(or_dev, row_dev, reflections_n, detector)
    evolved = jnp.einsum("okf,kod,orkd->kfrd", frame_pick, band_mask, projected)
    ordered = evolved.reshape(images_n, row_dev, detector)[slot_image]
    owned = lax.psum_scatter(ordered, "orient", scatter_dimension=0, tiled=True)
    residual = measured - owned
    everyone = lax.all_gather(residual.astype(jnp.bfloat16), "orient", axis=0, tiled=True)
    by_image = everyone[inverse].reshape(reflections_n, FRAMES, row_dev, detector)
    picked = by_image[reflections[None, :], frame_of]
    masked = picked * jnp.transpose(band_mask, (1, 0, 2))[:, :, None, :].astype(jnp.bfloat16)
    gradient = jnp.einsum("okrd,ckd->orc", masked, rays, preferred_element_type=jnp.float32)
    step_gain = math.sqrt(cell_count * orients_all / (FRAMES * reflections_n * detector))
    density = volume.astype(jnp.float32) + relax[:, None, None] * step_gain * gradient
    total_rows = row_dev * lax.axis_size("slab")
    base_row = lax.axis_index("slab") * row_dev
    for repeat in range(SWEEPS):
        extended = extended_2(density, (("slab", 1),), 1)
        density = smooth_pass(extended, base_row - 1, total_rows)
    return (density.astype(jnp.bfloat16), residual)


def solution(mesh):
    placed = (
        P("orient", "slab", None),
        P(),
        P(None, "orient"),
        P(None, "orient"),
        P(),
        P("orient", "slab", None),
        P("orient"),
    )
    return jax.shard_map(
        local,
        mesh=mesh,
        in_specs=placed,
        out_specs=(P("orient", "slab", None), P("orient", "slab", None)),
        check_vma=False,
    )
```

profile of v0, /device:TPU:24, one launch (start us, length us, event | category | flops | bytes accessed | tf_op | source)
XLA Modules:
  0.0 423.2 jit_solution(1588492112718736785)
XLA Ops:
  7.2 0.0 reduce-scatter.2.cloned.1.call-start
  7.2 15.6 %copy.30 = bf16[1024,8,8,128]{3,1,2,0:T(8,128)(2,1)} copy(bf16[1024,8,8,128]{3,2,1,0:T(8,128)(2,1)} %bitcast.48) | data formatting | bytes 33554432
  22.8 21.1 %copy.15 = bf16[1024,8192]{1,0:T(8,128)(2,1)} copy(bf16[1024,8192]{0,1:T(8,128)(2,1)} %bitcast.47) | data formatting | bytes 33554432 | tf_op jit(solution)/shard_map/dot_general | solution.py:62
  43.9 0.0 copy-done.1
  43.9 0.1 fusion.46
  44.0 8.1 %fusion.38 = f32[8,128,128]{1,2,0:T(8,128)S(1)} fusion(bf16[8,128,8192]{2,1,0:T(8,128)(2,1)} %bitcast.49, bf16[1,128,8192]{2,1,0:T(8,128)(2,1)S(1)} %copy-done.2, f32[8,128]{1,0:T(8,128)S(1)} %get-tuple-element.9), kind=kOutput, calls=%fused_computation.37 | convolution fusion | flops 2147614720 | bytes 19402752 | tf_op jit(solution)/shard_map/dot_general | solution.py:62
  52.2 0.2 copy.16
  52.4 0.1 fusion.43
  52.5 0.0 copy-start
  52.5 0.2 broadcast_multiply_fusion
  52.7 2.0 gather_fusion
  54.7 0.0 reduce-scatter.2.cloned.1.call-update
  54.7 0.0 all-gather.2.cloned.1.call-start
  54.8 162.5 %reduce-scatter.2.cloned.1.call-done = f32[1,128,128]{2,1,0:T(8,128)} async-done(((f32[32,128,128]{2,1,0:T(8,128)}), f32[1,128,128]{2,1,0:T(8,128)}) %reduce-scatter.2.cloned.1.call-update) | async-done | bytes 65552 | tf_op jit(solution)/shard_map/reduce_scatter | solution.py:68
  217.3 1.5 fusion.53
  218.8 0.0 all-gather.2.cloned.1.call-update
  219.4 0.7 scatter_custom_fusion
  220.2 151.0 %all-gather.2.cloned.1.call-done = bf16[32,128,128]{2,1,0:T(8,128)(2,1)} async-done(((bf16[1,128,128]{2,1,0:T(8,128)(2,1)}), bf16[32,128,128]{2,1,0:T(8,128)(2,1)}) %all-gather.2.cloned.1.call-update) | async-done | bytes 1048592 | tf_op jit(solution)/shard_map/all_gather | solution.py:70
  371.2 2.0 gather_fusion.1
  373.2 0.6 gather_fusion.2
  373.8 14.0 %fusion.11 = f32[1,128,8192]{2,1,0:T(8,128)} fusion(bf16[8192,8,128]{2,1,0:T(8,128)(2,1)} %param.8, bf16[1,128,8192]{2,1,0:T(8,128)(2,1)} %param.7, f32[]{:T(128)} %bitcast, bf16[8,128,128]{2,1,0:T(8,128)(2,1)S(1)} %gather_fusion.2, bf16[8,128]{1,0:T(8,128)(2,1)S(1)} %get-tuple-element.8), kind=kOutput, calls=%fused_computation.10 | convolution fusion | flops 2150760448 | bytes 23332868 | tf_op jit(solution)/shard_map/okrd,ckd->orc/dot_general | solution.py:74
  387.8 1.1 fusion.55
  388.8 1.9 collective-permute-start.1
  390.8 2.4 collective-permute-start
  393.2 0.0 collective-permute-done.1
  393.2 4.3 %collective-permute-done = f32[1,1,8192]{2,1,0:T(1,128)S(1)} collective-permute-done((f32[1,1,8192]{2,1,0:T(1,128)S(1)}, f32[1,1,8192]{2,1,0:T(1,128)S(1)}, u32[]{:S(2)}, u32[]{:S(2)}) %collective-permute-start) | collective-permute-done | bytes 32800 | tf_op jit(solution)/shard_map/ppermute | solution.py:24
  397.5 6.0 %fusion.29 = f32[1,128,8192]{2,1,0:T(8,128)S(1)} fusion(f32[1,128,8192]{2,1,0:T(8,128)} %fusion.11, f32[1,1,8192]{2,1,0:T(1,128)S(1)} %collective-permute-done.1, f32[1,1,8192]{2,1,0:T(1,128)S(1)} %collective-permute-done, pred[128]{0:T(512)(128)(4,1)S(1)} %get-tuple-element.10, pred[128]{0:T(512)(128)(4,1)S(1)} %get-tuple-element.11), kind=kLoop, calls=%fused_computation.29 | loop fusion | flops 11534336 | bytes 8454400 | tf_op jit(solution)/shard_map/sub | solution.py:42
  403.6 1.9 collective-permute-start.3
  405.5 2.4 collective-permute-start.2
  407.9 0.0 collective-permute-done.3
  407.9 4.3 %collective-permute-done.2 = f32[1,1,8192]{2,1,0:T(1,128)S(1)} collective-permute-done((f32[1,1,8192]{2,1,0:T(1,128)S(1)}, f32[1,1,8192]{2,1,0:T(1,128)S(1)}, u32[]{:S(2)}, u32[]{:S(2)}) %collective-permute-start.2) | collective-permute-done | bytes 32800 | tf_op jit(solution)/shard_map/ppermute | solution.py:24
  412.2 4.2 fusion.20
  (21 shorter events, 0.1 us)
Async XLA Ops:
  7.2 210.1 %reduce-scatter.2.cloned.1.call-start = ((), (), s32[]{:S(2)}) async-start(), calls=%async_computation.1 | async-start | bytes 2162688 | tf_op jit(solution)/shard_map/reduce_scatter | solution.py:68
  22.8 21.1 %copy-start.1 = (s32[8,1]{0,1:T(1,128)S(1)}, s32[8,1]{0,1:T(1,128)}, u32[]{:S(2)}) copy-start(s32[8,1]{0,1:T(1,128)} %param.9) | copy-start | bytes 100
  22.8 21.1 %copy-start.3 = (s32[8,1]{0,1:T(1,128)S(1)}, s32[8,1]{0,1:T(1,128)}, u32[]{:S(2)}) copy-start(s32[8,1]{0,1:T(1,128)} %param.10) | copy-start | bytes 100
  22.8 21.2 %copy-start.2 = (bf16[1,128,8192]{2,1,0:T(8,128)(2,1)S(1)}, bf16[1,128,8192]{2,1,0:T(8,128)(2,1)}, u32[]{:S(2)}) copy-start(bf16[1,128,8192]{2,1,0:T(8,128)(2,1)} %param.7) | copy-start | bytes 6291460
  44.0 8.4 %copy-start.4 = (s32[32]{0:T(128)S(1)}, s32[32]{0:T(128)}, u32[]{:S(2)}) copy-start(s32[32]{0:T(128)} %param.11) | copy-start | bytes 388
  52.5 164.8 %copy-start = (f32[1,128,128]{2,1,0:T(8,128)S(1)}, f32[1,128,128]{2,1,0:T(8,128)}, u32[]{:S(2)}) copy-start(f32[1,128,128]{2,1,0:T(8,128)} %param.12) | copy-start | bytes 196612
  54.7 316.5 %all-gather.2.cloned.1.call-start = ((), (), s32[]{:S(2)}) async-start(), calls=%async_computation.2 | async-start | bytes 1081344 | tf_op jit(solution)/shard_map/all_gather | solution.py:70
  388.8 4.4 %collective-permute-start.1 = (f32[1,1,8192]{2,1,0:T(1,128)S(1)}, f32[1,1,8192]{2,1,0:T(1,128)S(1)}, u32[]{:S(2)}, u32[]{:S(2)}) collective-permute-start(f32[1,1,8192]{2,1,0:T(1,128)S(1)} %get-tuple-element.7), channel_id=1, source_target_pairs={{1,0},{2,1},{3,2},{5,4},{6,5},{7,6},{9,8},{10,9},{11,10},{13,12},{... | collective-permute-start | bytes 98312 | tf_op jit(solution)/shard_map/ppermute | solution.py:26
  390.8 6.7 %collective-permute-start = (f32[1,1,8192]{2,1,0:T(1,128)S(1)}, f32[1,1,8192]{2,1,0:T(1,128)S(1)}, u32[]{:S(2)}, u32[]{:S(2)}) collective-permute-start(f32[1,1,8192]{2,1,0:T(1,128)S(1)} %get-tuple-element.6), channel_id=1, source_target_pairs={{0,1},{1,2},{2,3},{4,5},{5,6},{6,7},{8,9},{9,10},{10,11},{12,13},{... | collective-permute-start | bytes 98312 | tf_op jit(solution)/shard_map/ppermute | solution.py:24
  403.6 4.3 %collective-permute-start.3 = (f32[1,1,8192]{2,1,0:T(1,128)S(1)}, f32[1,1,8192]{2,1,0:T(1,128)S(1)}, u32[]{:S(2)}, u32[]{:S(2)}) collective-permute-start(f32[1,1,8192]{2,1,0:T(1,128)S(1)} %get-tuple-element.5), channel_id=1, source_target_pairs={{1,0},{2,1},{3,2},{5,4},{6,5},{7,6},{9,8},{10,9},{11,10},{13,12},{... | collective-permute-start | bytes 98312 | tf_op jit(solution)/shard_map/ppermute | solution.py:26
  405.5 6.7 %collective-permute-start.2 = (f32[1,1,8192]{2,1,0:T(1,128)S(1)}, f32[1,1,8192]{2,1,0:T(1,128)S(1)}, u32[]{:S(2)}, u32[]{:S(2)}) collective-permute-start(f32[1,1,8192]{2,1,0:T(1,128)S(1)} %get-tuple-element.4), channel_id=1, source_target_pairs={{0,1},{1,2},{2,3},{4,5},{5,6},{6,7},{8,9},{9,10},{10,11},{12,13},{... | collective-permute-start | bytes 98312 | tf_op jit(solution)/shard_map/ppermute | solution.py:24
Sparse Core Ops, SparseCore 0:
  54.9 162.3 reduce-scatter.1
  219.5 151.6 all-gather.1
where the time goes:
time: 425 us; the launch traced here: 423 us
  waiting for transfers between devices  322 us (76%)
  local copies, waits for them, and re-layouts  43.3 us (10%)
  matrix products  22.1 us (5%)
  between operations  14.9 us (4%)
  other arithmetic  12.1 us (3%)
  starting transfers between devices  8.73 us (2%)
    reduce_scatter x1, waiting for transfers between devices, local(): owned = lax.psum_scatter(ordered, 'orient', scatter_dimension=0, tiled=True)  162 us
    all_gather x1, waiting for transfers between devices, local(): lax.all_gather(residual.astype(jnp.bfloat16), 'orient', axis=0, tiled=True)  151 us
    dot_general x1, local copies, waits for them, and re-layouts, local(): jnp.dot(volume.reshape(or_dev * row_dev, cell_count), flat_rays, preferre...  21.1 us
    unnamed x11, local copies, waits for them, and re-layouts  15.6 us
    dot_general x1, matrix products, local(): jnp.einsum('okrd,ckd->orc', masked, rays, preferred_element_type=jnp.floa...  14 us
    ppermute x2, waiting for transfers between devices, extended_2(): lax.ppermute(tail, axis, [(i, (i + 1) % count) for i in range(ends)])  8.62 us
  transfers between devices with their start and end apart: 6, of which 4 were waited for; matrix products, arithmetic and copies ran while one was open for 0% of the time, Pallas kernels for 0%

commit v1 on v0

v1 whole, which is shorter than its diff:
```python
import math

import jax
import jax.numpy as jnp
from jax import lax
from jax.experimental import pallas as pl
from jax.experimental.pallas import tpu as pltpu
from jax.sharding import PartitionSpec as P

FRAMES = 4
SWEEPS = 2
HALO = 16

huber_delta = 0.5
sweep_rate = 0.2

bf16 = jnp.bfloat16
f32 = jnp.float32


def project_kernel(vol_hbm, halo_ref, rays_hbm, mask_ref, proj_ref, flat_ref, vol_ref, buf, acc, vsem, rsem):
    chunk = buf.shape[0] // rsem.shape[0]
    chunks = rsem.shape[0]
    rows = vol_hbm.shape[0]
    refl, det = rays_hbm.shape[1:]

    def rays_copy(i):
        at = pl.ds(pl.multiple_of(i * chunk, chunk), chunk)
        return pltpu.make_async_copy(rays_hbm.at[at], buf.at[at], rsem.at[i])

    def vol_copy(i):
        at = pl.ds(pl.multiple_of(i * chunk, chunk), chunk)
        return pltpu.make_async_copy(vol_hbm.at[:, at], vol_ref.at[0:rows, at], vsem.at[i])

    for i in range(chunks):
        vol_copy(i).start()
        rays_copy(i).start()
    vol_ref[rows:, :] = halo_ref[...]
    acc[...] = jnp.zeros_like(acc)

    def step(i, carry):
        at = pl.ds(pl.multiple_of(i * chunk, chunk), chunk)
        vol_copy(i).wait()
        rays_copy(i).wait()
        flat = buf[at].reshape(chunk, refl * det)
        flat_ref[at, :] = flat
        acc[...] += jnp.dot(vol_ref[:, at], flat, preferred_element_type=f32)
        return carry

    lax.fori_loop(0, chunks, step, 0)
    for k in range(refl):
        proj_ref[k] = acc[:, k * det : (k + 1) * det] * mask_ref[k : k + 1, :]


def project(vol, halo, rays, mask, chunk=1024):
    rows, cells = vol.shape
    refl, det = rays.shape[1:]
    ext = rows + HALO
    vmem = pl.BlockSpec(memory_space=pltpu.VMEM)
    hbm = pl.BlockSpec(memory_space=pltpu.HBM)
    return pl.pallas_call(
        project_kernel,
        in_specs=[hbm, vmem, hbm, vmem],
        out_specs=(vmem, vmem, vmem),
        out_shape=(
            jax.ShapeDtypeStruct((refl, ext, det), f32),
            pltpu.VMEM((cells, refl * det), bf16),
            pltpu.VMEM((ext, cells), bf16),
        ),
        scratch_shapes=[
            pltpu.VMEM(rays.shape, bf16),
            pltpu.VMEM((ext, refl * det), f32),
            pltpu.SemaphoreType.DMA((cells // chunk,)),
            pltpu.SemaphoreType.DMA((cells // chunk,)),
        ],
        compiler_params=pltpu.CompilerParams(vmem_limit_bytes=24 << 20),
        name="project",
    )(vol, halo, rays, mask)


def update_kernel(img_ref, mask_ref, flat_ref, vol_ref, bound_ref, scale_ref, out_hbm, obuf, osem):
    refl = img_ref.shape[0]
    ext, cells = vol_ref.shape
    rows, chunk = obuf.shape[1:]
    img = jnp.concatenate([img_ref[k] * mask_ref[k : k + 1, :] for k in range(refl)], axis=1)
    bound = bound_ref[:, :1]
    scale = scale_ref[0]

    def out_copy(i, slot):
        at = pl.ds(pl.multiple_of(i * chunk, chunk), chunk)
        return pltpu.make_async_copy(obuf.at[slot], out_hbm.at[:, at], osem.at[slot])

    def step(i, carry):
        at = pl.ds(pl.multiple_of(i * chunk, chunk), chunk)
        slot = lax.rem(i, 2)
        gradient = lax.dot_general(
            img, flat_ref[at, :], (((1,), (1,)), ((), ())), preferred_element_type=f32
        )
        density = vol_ref[:, at].astype(f32) + scale * gradient
        for _ in range(SWEEPS):
            flux = pltpu.roll(density, ext - 1, 0) - density
            flux = jnp.minimum(jnp.maximum(flux, -bound), bound)
            density = density + sweep_rate * (flux - pltpu.roll(flux, 1, 0))

        @pl.when(i >= 2)
        def _():
            out_copy(i - 2, slot).wait()

        obuf[slot] = density[:rows].astype(bf16)
        out_copy(i, slot).start()
        return carry

    steps = cells // chunk
    lax.fori_loop(0, steps, step, 0)
    for i in range(steps - 2, steps):
        out_copy(i, i % 2).wait()


def update(img, mask, flat, vol_ext, bound, scale, chunk=1024):
    ext, cells = vol_ext.shape
    rows = ext - HALO
    vmem = pl.BlockSpec(memory_space=pltpu.VMEM)
    return pl.pallas_call(
        update_kernel,
        in_specs=[vmem] * 5 + [pl.BlockSpec(memory_space=pltpu.SMEM)],
        out_specs=pl.BlockSpec(memory_space=pltpu.HBM),
        out_shape=jax.ShapeDtypeStruct((rows, cells), bf16),
        scratch_shapes=[pltpu.VMEM((2, rows, chunk), bf16), pltpu.SemaphoreType.DMA((2,))],
        compiler_params=pltpu.CompilerParams(vmem_limit_bytes=24 << 20),
        name="update",
    )(img, mask, flat, vol_ext, bound, scale)


def local(volume, rays, band_start, band_len, slot_image, measured, relax):
    cells, refl, det = rays.shape
    rows = volume.shape[1]
    slabs = lax.axis_size("slab")
    orients = lax.axis_size("orient")
    orient = lax.axis_index("orient")
    slab = lax.axis_index("slab")
    members = orients // FRAMES
    classes = [[g * FRAMES + q for g in range(members)] for q in range(FRAMES)]
    vol = volume[0]
    meas = measured[0].astype(bf16)

    edge = jnp.concatenate([vol, meas], axis=1)
    above = lax.ppermute(edge[rows - 2 :], "slab", [(i, i + 1) for i in range(slabs - 1)])
    below = lax.ppermute(edge[:2], "slab", [(i + 1, i) for i in range(slabs - 1)])
    halo = jnp.concatenate([below, jnp.zeros((HALO - 4, cells + det), bf16), above], axis=0)
    meas_ext = jnp.concatenate([meas, halo[:, cells:]], axis=0)

    gathered = [meas_ext] + [
        lax.ppermute(meas_ext, "orient", [(o, o ^ s) for o in range(orients)]) for s in range(1, FRAMES)
    ]

    columns = jnp.arange(det, dtype=jnp.int32)
    inside = (columns >= band_start) & (columns < band_start + band_len)
    mask = inside.astype(f32)
    proj, flat, vol_ext = project(vol, halo[:, :cells], rays, mask)

    reflections = jnp.arange(refl, dtype=jnp.int32)
    wanted = reflections * FRAMES + (orient + reflections) % FRAMES
    part = proj
    for s in range(FRAMES):
        held = (wanted == slot_image[orient ^ s]).astype(f32)
        part = part - held[:, None, None] * gathered[s].astype(f32)[None]
    pieces = lax.all_to_all(
        part.astype(bf16), "orient", 0, 0, axis_index_groups=classes, tiled=True
    )
    own = (-jnp.sum(pieces.astype(f32), axis=0)).astype(bf16)
    images = lax.all_to_all(
        jnp.broadcast_to(own[None], (members, rows + HALO, det)),
        "orient", 0, 0, axis_index_groups=classes, tiled=True,
    )

    mine = slot_image[orient]
    source = ((mine % FRAMES - mine // FRAMES) ^ orient) % FRAMES
    residual = images[mine // FRAMES, :rows]
    for s in range(1, FRAMES):
        sent = images[slot_image[orient ^ s] // FRAMES, :rows]
        got = lax.ppermute(sent, "orient", [(o, o ^ s) for o in range(orients)])
        residual = jnp.where(source == s, got, residual)

    step_gain = math.sqrt(cells * orients / (FRAMES * refl * det))
    place = jnp.arange(rows + HALO, dtype=jnp.int32)[:, None]
    last = (place == rows - 1) & (slab == slabs - 1)
    first = (place == rows + HALO - 1) & (slab == 0)
    bound = jnp.broadcast_to(jnp.where(last | first, 0.0, huber_delta), (rows + HALO, det))
    updated = update(images, mask.astype(bf16), flat, vol_ext, bound, relax * step_gain)
    return (updated[None], residual.astype(f32)[None])


def solution(mesh):
    placed = (
        P("orient", "slab", None),
        P(),
        P(None, "orient"),
        P(None, "orient"),
        P(),
        P("orient", "slab", None),
        P("orient"),
    )
    return jax.shard_map(
        local,
        mesh=mesh,
        in_specs=placed,
        out_specs=(P("orient", "slab", None), P("orient", "slab", None)),
        check_vma=False,
    )
```

time: 425 us -> 91 us (0.21)
  waiting for transfers between devices: 322 us -> 0.52 us
  local copies, waits for them, and re-layouts: 43.3 us -> 15.3 us
  matrix products: 22.1 us -> 0 us
  Pallas kernels: 0 us -> 20.8 us
  blocking collectives: 0 us -> 16.7 us
  starting transfers between devices: 8.73 us -> 17.6 us
  other arithmetic: 12.1 us -> 7.34 us
    reduce_scatter x1 -> x0, waiting for transfers between devices: 162 us -> none  [local(): owned = lax.psum_scatter(ordered, 'orient', scatter_dimension=0, tiled=True)]
    all_gather x1 -> x0, waiting for transfers between devices: 151 us -> none  [local(): lax.all_gather(residual.astype(jnp.bfloat16), 'orient', axis=0, tiled=True)]
    dot_general x2 -> x0, matrix products: 22.1 us -> none  [the longest x1 14 us: local(): jnp.einsum('okrd,ckd->orc', masked, rays, preferred_element_type=jnp.floa...]
    dot_general x1 -> x0, local copies, waits for them, and re-layouts: 21.1 us -> none  [local(): jnp.dot(volume.reshape(or_dev * row_dev, cell_count), flat_rays, preferre...]
    pallas_call x0 -> x2, Pallas kernels: none -> 20.8 us  [the longest x1 11.1 us: update(): pl.pallas_call(update_kernel, in_specs=[vmem] * 5 + [pl.BlockSpec(memory_...]
    all_to_all x0 -> x1, blocking collectives: none -> 16.7 us  [local(): lax.all_to_all(part.astype(bf16), 'orient', 0, 0, axis_index_groups=class...]
    ppermute x4 -> x8, waiting for transfers between devices: 8.62 us -> 0.02 us  [the longest x3 0.01 us: local(): lax.ppermute(meas_ext, 'orient', [(o, o ^ s) for o in range(orients)])]
    sub x1 -> x0, other arithmetic: 6 us -> none  [smooth_pass(): return middle - sweep_rate * row_flux]
  transfers between devices with their start and end apart: 6 -> 9, of which waited for: 4 -> 1; matrix products, arithmetic and copies ran while one was open for 0% -> 6% of each run, Pallas kernels for 0% -> 23%
where the time goes in v1:
time: 91 us; the launch traced here: 90.4 us
  Pallas kernels  20.8 us (23%)
  starting transfers between devices  17.6 us (19%)
  blocking collectives  16.7 us (18%)
  local copies, waits for them, and re-layouts  15.3 us (17%)
  between operations  12.2 us (13%)
  other arithmetic  7.34 us (8%)
    all_to_all x1, blocking collectives, local(): lax.all_to_all(part.astype(bf16), 'orient', 0, 0, axis_index_groups=class...  16.7 us
    unnamed x10, local copies, waits for them, and re-layouts  12.9 us
    pallas_call x1, Pallas kernels, update(): pl.pallas_call(update_kernel, in_specs=[vmem] * 5 + [pl.BlockSpec(memory_...  11.1 us
    pallas_call x1, Pallas kernels, project(): pl.pallas_call(project_kernel, in_specs=[hbm, vmem, hbm, vmem], out_specs...  9.67 us
    ppermute x1, starting transfers between devices, local(): lax.ppermute(edge[:2], 'slab', [(i + 1, i) for i in range(slabs - 1)])  5.15 us
    ppermute x3, starting transfers between devices, local(): got = lax.ppermute(sent, 'orient', [(o, o ^ s) for o in range(orients)])  3.57 us
    ppermute x3, starting transfers between devices, local(): lax.ppermute(meas_ext, 'orient', [(o, o ^ s) for o in range(orients)])  3.57 us
    all_to_all x1, starting transfers between devices, local(): lax.all_to_all(jnp.broadcast_to(own[None], (members, rows + HALO, det)),...  3.42 us
  transfers between devices with their start and end apart: 9, of which 1 were waited for; matrix products, arithmetic and copies ran while one was open for 6% of the time, Pallas kernels for 23%

profile of v1, /device:TPU:24, one launch (start us, length us, event | category | flops | bytes accessed | tf_op | source)
XLA Modules:
  0.0 90.4 jit_solution(4296331591684404947)
XLA Ops:
  0.6 0.0 copy-start.2
  0.6 1.0 %convert_bitcast_fusion = bf16[128,128]{1,0:T(8,128)(2,1)S(1)} fusion(f32[1,128,128]{2,1,0:T(8,128)} %param.12), kind=kLoop, calls=%fused_computation.14 | loop fusion | flops 16384 | bytes 98304 | tf_op jit(solution)/shard_map/convert_element_type | solution.py:144
  1.6 1.0 %pad_maximum_fusion.3 = (bf16[2,8320]{1,0:T(2,128)(2,1)S(1)}, bf16[2,8320]{1,0:T(2,128)(2,1)S(1)}) fusion(bf16[128,128]{1,0:T(8,128)(2,1)S(1)} %convert_bitcast_fusion, bf16[128,8192]{1,0:T(8,128)(2,1)} %bitcast.28), kind=kLoop, calls=%fused_computation.6 | loop fusion | flops 133120 | bytes 2196480 | tf_op jit(solution)/shard_map/slice | solution.py:148
  2.7 1.9 %collective-permute-start.1 = (bf16[2,8320]{1,0:T(2,128)(2,1)S(1)}, bf16[2,8320]{1,0:T(2,128)(2,1)S(1)}, u32[]{:S(2)}, u32[]{:S(2)}) collective-permute-start(bf16[2,8320]{1,0:T(2,128)(2,1)S(1)} %get-tuple-element.9), channel_id=1, source_target_pairs={{0,1},{1,2},{2,3},{4,5},{5,6},{6,7},{8,9},{9,10},{10,11},{12,13},{... | collective-permute-start | bytes 99848 | tf_op jit(solution)/shard_map/ppermute | solution.py:147
  4.6 5.1 %collective-permute-start = (bf16[2,8320]{1,0:T(2,128)(2,1)S(1)}, bf16[2,8320]{1,0:T(2,128)(2,1)S(1)}, u32[]{:S(2)}, u32[]{:S(2)}) collective-permute-start(bf16[2,8320]{1,0:T(2,128)(2,1)S(1)} %get-tuple-element.8), channel_id=1, source_target_pairs={{1,0},{2,1},{3,2},{5,4},{6,5},{7,6},{9,8},{10,9},{11,10},{13,12},{... | collective-permute-start | bytes 99848 | tf_op jit(solution)/shard_map/ppermute | solution.py:148
  9.8 0.7 add_bitcast_fusion
  10.4 0.7 fusion.4
  11.2 1.5 %fusion.8 = (s32[1]{0:T(128)}, s32[1]{0:T(128)}, s32[1]{0:T(128)}, s32[1]{0:T(128)}) fusion(s32[32]{0:T(128)} %param.11, s32[]{:T(128)S(6)} %select_n.102, s32[]{:T(128)S(6)} %select_n.103, s32[]{:T(128)S(6)} %select_n.105, s32[]{:T(128)S(6)} %select_n.104), kind=kLoop, calls=%fused_computation.32 | loop fusion | bytes 48 | tf_op jit(solution)/shard_map/dynamic_slice | solution.py:165
  12.6 1.3 %compare_convert_fusion = (f32[8]{0:T(128)S(1)}, f32[8]{0:T(128)S(1)}) fusion(s32[]{:T(128)} %bitcast.7, s32[]{:T(128)S(6)} %axis_index.23, s32[]{:T(128)} %bitcast.6), kind=kLoop, calls=%fused_computation.22 | loop fusion | flops 144 | bytes 76 | tf_op jit(solution)/shard_map/convert_element_type | solution.py:165
  14.0 0.1 pad.3.clone
  14.0 0.0 collective-permute-done.1
  14.1 0.1 pad_maximum_fusion
  14.2 2.2 %collective-permute-start.4 = (bf16[144,128]{1,0:T(8,128)(2,1)S(1)}, bf16[144,128]{1,0:T(8,128)(2,1)S(1)}, u32[]{:S(2)}, u32[]{:S(2)}) collective-permute-start(bf16[144,128]{1,0:T(8,128)(2,1)S(1)} %get-tuple-element.14), channel_id=1, source_target_pairs={{0,12},{4,8},{8,4},{12,0},{16,28},{20,24},{24,20},{28,16},{32,44},... | collective-permute-start | bytes 110600 | tf_op jit(solution)/shard_map/ppermute | solution.py:153
  16.4 0.1 collective-permute-start.3
  16.5 1.3 %collective-permute-start.2 = (bf16[144,128]{1,0:T(8,128)(2,1)S(1)}, bf16[144,128]{1,0:T(8,128)(2,1)S(1)}, u32[]{:S(2)}, u32[]{:S(2)}) collective-permute-start(bf16[144,128]{1,0:T(8,128)(2,1)S(1)} %get-tuple-element.14), channel_id=1, source_target_pairs={{0,4},{4,0},{8,12},{12,8},{16,20},{20,16},{24,28},{28,24},{32,36},... | collective-permute-start | bytes 110600 | tf_op jit(solution)/shard_map/ppermute | solution.py:153
  17.8 1.3 %compare_convert_fusion.2 = (f32[8]{0:T(128)S(1)}, f32[8]{0:T(128)S(1)}) fusion(s32[]{:T(128)} %bitcast.5, s32[]{:T(128)S(6)} %axis_index.23, s32[]{:T(128)} %bitcast.4), kind=kLoop, calls=%fused_computation.24 | loop fusion | flops 144 | bytes 76 | tf_op jit(solution)/shard_map/convert_element_type | solution.py:165
  19.1 9.7 %project.1 = (f32[8,144,128]{2,1,0:T(8,128)S(1)}, bf16[8192,1024]{1,0:T(8,128)(2,1)S(1)}, bf16[144,8192]{1,0:T(8,128)(2,1)S(1)}) custom-call(bf16[128,8192]{1,0:T(8,128)(2,1)S(1)} %bitcast.29, bf16[16,8192]{1,0:T(8,128)(2,1)S(1)} %slice.16.halo_ref, bf16[8192,8,128]{2,1,0:T(8,128)(2,1)} %rays_hbm.1, f32[8,128]{1,0:T(8,128)S(1)} %get-tuple-element.16.mask_ref), custom_call_target="tpu_custom_call" | custom-call | tf_op jit(solution)/shard_map/project/pallas_call | solution.py:61
  28.8 5.7 %copy-done = bf16[8192,1024]{1,0:T(8,128)(2,1)} copy-done((bf16[8192,1024]{1,0:T(8,128)(2,1)}, bf16[8192,1024]{1,0:T(8,128)(2,1)S(1)}, u32[]{:S(2)}) %copy-start) | copy-done | bytes 16777240
  34.5 1.4 %copy-done.3 = bf16[144,8192]{1,0:T(8,128)(2,1)} copy-done((bf16[144,8192]{1,0:T(8,128)(2,1)}, bf16[144,8192]{1,0:T(8,128)(2,1)S(1)}, u32[]{:S(2)}) %copy-start.3) | copy-done | bytes 2359320
  36.0 0.4 subtract_convert_fusion
  36.5 16.7 %all_to_all.10 = bf16[8,144,128]{2,1,0:T(8,128)(2,1)S(1)} all-to-all(bf16[8,144,128]{2,1,0:T(8,128)(2,1)S(1)} %subtract_convert_fusion), channel_id=1, replica_groups={{0,16,32,48,64,80,96,112},{4,20,36,52,68,84,100,116},{8,24,40,56,72,88,..., dimensions={0} | all-to-all | bytes 589824 | tf_op jit(solution)/shard_map/all_to_all | solution.py:167
  53.2 0.8 broadcast_in_dim.22
  53.9 3.4 %all-to-all-start.1 = ((bf16[8,144,128]{2,1,0:T(8,128)(2,1)}), bf16[8,144,128]{2,1,0:T(8,128)(2,1)S(1)}, u32[]{:S(2)}, u32[]{:S(2)}) async-start(bf16[8,144,128]{2,1,0:T(8,128)(2,1)} %broadcast_in_dim.22), calls=%async_computation.1 | async-start | bytes 589824 | tf_op jit(solution)/shard_map/all_to_all | solution.py:171
  65.4 0.5 all-to-all-done.1.img_ref
  65.9 1.6 %collective-permute-start.5 = (bf16[128,128]{1,0:T(8,128)(2,1)S(1)}, bf16[128,128]{1,0:T(8,128)(2,1)S(1)}, u32[]{:S(2)}, u32[]{:S(2)}) collective-permute-start(bf16[128,128]{1,0:T(8,128)(2,1)S(1)} %get-tuple-element.12), channel_id=1, source_target_pairs={{0,12},{4,8},{8,4},{12,0},{16,28},{20,24},{24,20},{28,16},{32,44},... | collective-permute-start | bytes 98312 | tf_op jit(solution)/shard_map/ppermute | solution.py:181
  67.5 0.7 collective-permute-start.6
  68.2 1.3 %collective-permute-start.7 = (bf16[128,128]{1,0:T(8,128)(2,1)S(1)}, bf16[128,128]{1,0:T(8,128)(2,1)S(1)}, u32[]{:S(2)}, u32[]{:S(2)}) collective-permute-start(bf16[128,128]{1,0:T(8,128)(2,1)S(1)} %get-tuple-element.10), channel_id=1, source_target_pairs={{0,4},{4,0},{8,12},{12,8},{16,20},{20,16},{24,28},{28,24},{32,36},... | collective-permute-start | bytes 98312 | tf_op jit(solution)/shard_map/ppermute | solution.py:181
  72.8 0.1 broadcast_in_dim.46.bound_ref
  72.8 0.0 copy-done.4
  72.8 5.8 %copy-done.1 = bf16[8192,1024]{1,0:T(8,128)(2,1)S(1)} copy-done((bf16[8192,1024]{1,0:T(8,128)(2,1)S(1)}, bf16[8192,1024]{1,0:T(8,128)(2,1)}, u32[]{:S(2)}) %copy-start.1) | copy-done | bytes 16777240
  78.6 11.1 %update.1 = bf16[128,8192]{1,0:T(8,128)(2,1)} custom-call(bf16[8,144,128]{2,1,0:T(8,128)(2,1)S(1)} %all-to-all-done.1.img_ref, bf16[8,128]{1,0:T(8,128)(2,1)S(1)} %get-tuple-element.15.mask_ref, bf16[8192,1024]{1,0:T(8,128)(2,1)S(1)} %copy-done.1, bf16[144,8192]{1,0:T(8,128)(2,1)S(1)} %copy-done.4, f32[144,128]{1,0:T(8,128)S(1)} %broadcast_in_dim.46.bound_ref, ...), custom_call_target="tpu_custom_call" | custom-call | tf_op jit(solution)/shard_map/update/pallas_call | solution.py:123
  89.8 0.6 bitcast_convert_fusion
  (23 shorter events, 0.1 us)
Async XLA Ops:
  0.6 18.5 %copy-start.2 = (bf16[1,128,8192]{2,1,0:T(8,128)(2,1)S(1)}, bf16[1,128,8192]{2,1,0:T(8,128)(2,1)}, u32[]{:S(2)}) copy-start(bf16[1,128,8192]{2,1,0:T(8,128)(2,1)} %param.7) | copy-start | bytes 6291460
  2.7 11.4 %collective-permute-start.1 = (bf16[2,8320]{1,0:T(2,128)(2,1)S(1)}, bf16[2,8320]{1,0:T(2,128)(2,1)S(1)}, u32[]{:S(2)}, u32[]{:S(2)}) collective-permute-start(bf16[2,8320]{1,0:T(2,128)(2,1)S(1)} %get-tuple-element.9), channel_id=1, source_target_pairs={{0,1},{1,2},{2,3},{4,5},{5,6},{6,7},{8,9},{9,10},{10,11},{12,13},{... | collective-permute-start | bytes 99848 | tf_op jit(solution)/shard_map/ppermute | solution.py:147
  4.6 9.5 %collective-permute-start = (bf16[2,8320]{1,0:T(2,128)(2,1)S(1)}, bf16[2,8320]{1,0:T(2,128)(2,1)S(1)}, u32[]{:S(2)}, u32[]{:S(2)}) collective-permute-start(bf16[2,8320]{1,0:T(2,128)(2,1)S(1)} %get-tuple-element.8), channel_id=1, source_target_pairs={{1,0},{2,1},{3,2},{5,4},{6,5},{7,6},{9,8},{10,9},{11,10},{13,12},{... | collective-permute-start | bytes 99848 | tf_op jit(solution)/shard_map/ppermute | solution.py:148
  14.2 21.8 %collective-permute-start.4 = (bf16[144,128]{1,0:T(8,128)(2,1)S(1)}, bf16[144,128]{1,0:T(8,128)(2,1)S(1)}, u32[]{:S(2)}, u32[]{:S(2)}) collective-permute-start(bf16[144,128]{1,0:T(8,128)(2,1)S(1)} %get-tuple-element.14), channel_id=1, source_target_pairs={{0,12},{4,8},{8,4},{12,0},{16,28},{20,24},{24,20},{28,16},{32,44},... | collective-permute-start | bytes 110600 | tf_op jit(solution)/shard_map/ppermute | solution.py:153
  16.4 19.6 %collective-permute-start.3 = (bf16[144,128]{1,0:T(8,128)(2,1)S(1)}, bf16[144,128]{1,0:T(8,128)(2,1)S(1)}, u32[]{:S(2)}, u32[]{:S(2)}) collective-permute-start(bf16[144,128]{1,0:T(8,128)(2,1)S(1)} %get-tuple-element.14), channel_id=1, source_target_pairs={{0,8},{4,12},{8,0},{12,4},{16,24},{20,28},{24,16},{28,20},{32,40},... | collective-permute-start | bytes 110600 | tf_op jit(solution)/shard_map/ppermute | solution.py:153
  16.5 19.5 %collective-permute-start.2 = (bf16[144,128]{1,0:T(8,128)(2,1)S(1)}, bf16[144,128]{1,0:T(8,128)(2,1)S(1)}, u32[]{:S(2)}, u32[]{:S(2)}) collective-permute-start(bf16[144,128]{1,0:T(8,128)(2,1)S(1)} %get-tuple-element.14), channel_id=1, source_target_pairs={{0,4},{4,0},{8,12},{12,8},{16,20},{20,16},{24,28},{28,24},{32,36},... | collective-permute-start | bytes 110600 | tf_op jit(solution)/shard_map/ppermute | solution.py:153
  28.8 5.7 %copy-start = (bf16[8192,1024]{1,0:T(8,128)(2,1)}, bf16[8192,1024]{1,0:T(8,128)(2,1)S(1)}, u32[]{:S(2)}) copy-start(bf16[8192,1024]{1,0:T(8,128)(2,1)S(1)} %get-tuple-element.6.flat_ref) | copy-start | bytes 50331652
  34.5 1.4 %copy-start.3 = (bf16[144,8192]{1,0:T(8,128)(2,1)}, bf16[144,8192]{1,0:T(8,128)(2,1)S(1)}, u32[]{:S(2)}) copy-start(bf16[144,8192]{1,0:T(8,128)(2,1)S(1)} %get-tuple-element.7.vol_ref) | copy-start | bytes 7077892
  36.0 36.9 %copy-start.4 = (bf16[144,8192]{1,0:T(8,128)(2,1)S(1)}, bf16[144,8192]{1,0:T(8,128)(2,1)}, u32[]{:S(2)}) copy-start(bf16[144,8192]{1,0:T(8,128)(2,1)} %copy-done.3) | copy-start | bytes 7077892
  53.9 11.9 %all-to-all-start.1 = ((bf16[8,144,128]{2,1,0:T(8,128)(2,1)}), bf16[8,144,128]{2,1,0:T(8,128)(2,1)S(1)}, u32[]{:S(2)}, u32[]{:S(2)}) async-start(bf16[8,144,128]{2,1,0:T(8,128)(2,1)} %broadcast_in_dim.22), calls=%async_computation.1 | async-start | bytes 589824 | tf_op jit(solution)/shard_map/all_to_all | solution.py:171
  65.9 23.9 %collective-permute-start.5 = (bf16[128,128]{1,0:T(8,128)(2,1)S(1)}, bf16[128,128]{1,0:T(8,128)(2,1)S(1)}, u32[]{:S(2)}, u32[]{:S(2)}) collective-permute-start(bf16[128,128]{1,0:T(8,128)(2,1)S(1)} %get-tuple-element.12), channel_id=1, source_target_pairs={{0,12},{4,8},{8,4},{12,0},{16,28},{20,24},{24,20},{28,16},{32,44},... | collective-permute-start | bytes 98312 | tf_op jit(solution)/shard_map/ppermute | solution.py:181
  67.5 22.3 %collective-permute-start.6 = (bf16[128,128]{1,0:T(8,128)(2,1)S(1)}, bf16[128,128]{1,0:T(8,128)(2,1)S(1)}, u32[]{:S(2)}, u32[]{:S(2)}) collective-permute-start(bf16[128,128]{1,0:T(8,128)(2,1)S(1)} %get-tuple-element.11), channel_id=1, source_target_pairs={{0,8},{4,12},{8,0},{12,4},{16,24},{20,28},{24,16},{28,20},{32,40},... | collective-permute-start | bytes 98312 | tf_op jit(solution)/shard_map/ppermute | solution.py:181
  68.2 21.6 %collective-permute-start.7 = (bf16[128,128]{1,0:T(8,128)(2,1)S(1)}, bf16[128,128]{1,0:T(8,128)(2,1)S(1)}, u32[]{:S(2)}, u32[]{:S(2)}) collective-permute-start(bf16[128,128]{1,0:T(8,128)(2,1)S(1)} %get-tuple-element.10), channel_id=1, source_target_pairs={{0,4},{4,0},{8,12},{12,8},{16,20},{20,16},{24,28},{28,24},{32,36},... | collective-permute-start | bytes 98312 | tf_op jit(solution)/shard_map/ppermute | solution.py:181
  72.8 5.8 %copy-start.1 = (bf16[8192,1024]{1,0:T(8,128)(2,1)S(1)}, bf16[8192,1024]{1,0:T(8,128)(2,1)}, u32[]{:S(2)}) copy-start(bf16[8192,1024]{1,0:T(8,128)(2,1)} %copy-done) | copy-start | bytes 50331652

commit v2 on v1

v2 whole, which is shorter than its diff:
```python
import math

import jax
import jax.numpy as jnp
from jax import lax
from jax.experimental import pallas as pl
from jax.experimental.pallas import tpu as pltpu
from jax.sharding import PartitionSpec as P

FRAMES = 4
SWEEPS = 2
HALO = 16

huber_delta = 0.5
sweep_rate = 0.2

bf16 = jnp.bfloat16
f32 = jnp.float32


SMALL = 4 << 20

MASK = 0
HELD = 8
PICK = 40
FROM = 72
SCALE = 76
BOUND = 77
TABLE = 80

VMEM = pl.BlockSpec(memory_space=pltpu.VMEM)
SMEM = pl.BlockSpec(memory_space=pltpu.SMEM)
HBM = pl.BlockSpec(memory_space=pltpu.HBM)


def keep(x):
    return pltpu.with_memory_space_constraint(x, pltpu.HBM)


def prepare_kernel(step_gain, slabs, vol_hbm, meas_hbm, start_hbm, len_hbm, slot_hbm, relax_ref,
                   low_ref, high_ref, meas_ref, table_ref,
                   first, last, start_ref, len_ref, slot_ref, sem):
    rows, cells = vol_hbm.shape
    det = meas_ref.shape[1]
    tile = first.shape[0]
    pairs = [
        (vol_hbm.at[0:tile], first),
        (vol_hbm.at[rows - tile : rows], last),
        (meas_hbm, meas_ref),
        (start_hbm, start_ref),
        (len_hbm, len_ref),
        (slot_hbm, slot_ref),
    ]
    copies = [pltpu.make_async_copy(*pair, sem.at[i]) for i, pair in enumerate(pairs)]
    for copy in copies:
        copy.start()
    for copy in copies:
        copy.wait()
    orient = lax.axis_index("orient")
    slab = lax.axis_index("slab")
    lanes = lax.broadcasted_iota(jnp.int32, (1, det), 1)

    def line(flag):
        return jnp.full((1, det), jnp.where(flag, 1.0, 0.0), f32)

    for k in range(8):
        begin = start_ref[k]
        inside = (lanes >= begin) & (lanes < begin + len_ref[k])
        table_ref[MASK + k : MASK + k + 1, :] = jnp.where(inside, 1.0, 0.0)
    for s in range(FRAMES):
        image = slot_ref[jnp.bitwise_xor(orient, s)]
        refl = jnp.right_shift(image, 2)
        for k in range(8):
            wanted = k * FRAMES + jnp.bitwise_and(orient + k, FRAMES - 1)
            table_ref[HELD + 8 * s + k : HELD + 8 * s + k + 1, :] = line(image == wanted)
            table_ref[PICK + 8 * s + k : PICK + 8 * s + k + 1, :] = line(refl == k)
    mine = slot_ref[orient]
    source = jnp.bitwise_and(jnp.bitwise_xor(mine - jnp.right_shift(mine, 2), orient), FRAMES - 1)
    for s in range(FRAMES):
        table_ref[FROM + s : FROM + s + 1, :] = line(source == s)
    table_ref[SCALE : SCALE + 1, :] = jnp.full((1, det), relax_ref[0] * step_gain, f32)
    table_ref[BOUND : BOUND + 1, :] = line(slab != slabs - 1) * huber_delta
    table_ref[BOUND + 1 : BOUND + 2, :] = line(slab != 0) * huber_delta
    table_ref[BOUND + 2 : BOUND + 3, :] = line(slab < 0)
    low_ref[:, cells:] = meas_ref[rows - 2 :, :].astype(bf16)
    high_ref[:, cells:] = meas_ref[0:2, :].astype(bf16)
    high_ref[:, 0:cells] = first[0:2, :]
    low_ref[:, 0:cells] = last[tile - 2 :, :]


def prepare(vol, start, length, slot_image, meas, relax, step_gain, slabs):
    rows, cells = vol.shape
    det = meas.shape[1]
    edge = jax.ShapeDtypeStruct((2, cells + det), bf16)
    return pl.pallas_call(
        lambda *refs: prepare_kernel(step_gain, slabs, *refs),
        in_specs=[HBM] * 5 + [SMEM],
        out_specs=(VMEM,) * 4,
        out_shape=(
            edge, edge, jax.ShapeDtypeStruct(meas.shape, f32), jax.ShapeDtypeStruct((TABLE, det), f32)
        ),
        scratch_shapes=[
            pltpu.VMEM((HALO, cells), bf16),
            pltpu.VMEM((HALO, cells), bf16),
            pltpu.SMEM(start.shape, jnp.int32),
            pltpu.SMEM(length.shape, jnp.int32),
            pltpu.SMEM(slot_image.shape, jnp.int32),
            pltpu.SemaphoreType.DMA((6,)),
        ],
        compiler_params=pltpu.CompilerParams(vmem_limit_bytes=SMALL),
        name="prepare",
    )(*(keep(x) for x in (vol, meas, start, length, slot_image)), relax)


def extend_kernel(meas_ref, below_ref, above_ref, ext_ref):
    rows, det = meas_ref.shape
    cells = below_ref.shape[1] - det
    ext_ref[0:rows] = meas_ref[...].astype(bf16)
    ext_ref[rows:] = jnp.concatenate(
        [below_ref[:, cells:], jnp.zeros((HALO - 4, det), bf16), above_ref[:, cells:]], axis=0
    )


def extend(meas, below, above):
    rows, det = meas.shape
    return pl.pallas_call(
        extend_kernel,
        in_specs=[VMEM] * 3,
        out_specs=VMEM,
        out_shape=jax.ShapeDtypeStruct((rows + HALO, det), bf16),
        compiler_params=pltpu.CompilerParams(vmem_limit_bytes=SMALL),
        name="extend",
    )(meas, below, above)


def project_kernel(vol_hbm, below_ref, above_ref, rays_hbm, table_ref, proj_ref, flat_ref, vol_ref, buf, acc, vsem, rsem):
    chunks = rsem.shape[0]
    chunk = buf.shape[0] // chunks
    rows, cells = vol_hbm.shape
    refl, det = rays_hbm.shape[1:]

    def rays_copy(i):
        at = pl.ds(pl.multiple_of(i * chunk, chunk), chunk)
        return pltpu.make_async_copy(rays_hbm.at[at], buf.at[at], rsem.at[i])

    def vol_copy(i):
        at = pl.ds(pl.multiple_of(i * chunk, chunk), chunk)
        return pltpu.make_async_copy(vol_hbm.at[:, at], vol_ref.at[0:rows, at], vsem.at[i])

    for i in range(chunks):
        vol_copy(i).start()
        rays_copy(i).start()
    vol_ref[rows:, :] = jnp.concatenate(
        [below_ref[:, 0:cells], jnp.zeros((HALO - 4, cells), bf16), above_ref[:, 0:cells]], axis=0
    )
    acc[...] = jnp.zeros_like(acc)

    def step(i, carry):
        at = pl.ds(pl.multiple_of(i * chunk, chunk), chunk)
        vol_copy(i).wait()
        rays_copy(i).wait()
        flat = buf[at].reshape(chunk, refl * det)
        flat_ref[at, :] = flat
        acc[...] += jnp.dot(vol_ref[:, at], flat, preferred_element_type=f32)
        return carry

    lax.fori_loop(0, chunks, step, 0)
    for k in range(refl):
        proj_ref[k] = acc[:, k * det : (k + 1) * det] * table_ref[MASK + k : MASK + k + 1, :]


def project(vol, below, above, rays, table, chunk=1024):
    rows, cells = vol.shape
    refl, det = rays.shape[1:]
    ext = rows + HALO
    return pl.pallas_call(
        project_kernel,
        in_specs=[HBM, VMEM, VMEM, HBM, VMEM],
        out_specs=(VMEM, VMEM, VMEM),
        out_shape=(
            jax.ShapeDtypeStruct((refl, ext, det), f32),
            pltpu.VMEM((cells, refl * det), bf16),
            pltpu.VMEM((ext, cells), bf16),
        ),
        scratch_shapes=[
            pltpu.VMEM(rays.shape, bf16),
            pltpu.VMEM((ext, refl * det), f32),
            pltpu.SemaphoreType.DMA((cells // chunk,)),
            pltpu.SemaphoreType.DMA((cells // chunk,)),
        ],
        compiler_params=pltpu.CompilerParams(vmem_limit_bytes=24 << 20),
        name="project",
    )(keep(vol), below, above, keep(rays), table)


def combine_kernel(proj_ref, table_ref, *refs):
    gathered, part_ref = refs[:FRAMES], refs[FRAMES]
    images = [ref[...].astype(f32) for ref in gathered]
    for k in range(proj_ref.shape[0]):
        part = proj_ref[k]
        for s in range(FRAMES):
            row = HELD + 8 * s + k
            part = part - table_ref[row : row + 1, :] * images[s]
        part_ref[k] = part.astype(bf16)


def combine(proj, table, gathered):
    return pl.pallas_call(
        combine_kernel,
        in_specs=[VMEM] * (2 + FRAMES),
        out_specs=VMEM,
        out_shape=jax.ShapeDtypeStruct(proj.shape, bf16),
        compiler_params=pltpu.CompilerParams(vmem_limit_bytes=SMALL),
        name="combine",
    )(proj, table, *gathered)


def total_kernel(pieces_ref, out_ref):
    count = pieces_ref.shape[0]
    total = pieces_ref[0].astype(f32)
    for i in range(1, count):
        total = total + pieces_ref[i].astype(f32)
    own = (-total).astype(bf16)
    for i in range(count):
        out_ref[i] = own


def total(pieces):
    return pl.pallas_call(
        total_kernel,
        in_specs=[VMEM],
        out_specs=VMEM,
        out_shape=jax.ShapeDtypeStruct(pieces.shape, bf16),
        compiler_params=pltpu.CompilerParams(vmem_limit_bytes=SMALL),
        name="total",
    )(pieces)


def pick_kernel(img_ref, table_ref, *outs):
    rows = outs[0].shape[0]
    for s in range(FRAMES):
        image = jnp.zeros(outs[0].shape, f32)
        for k in range(img_ref.shape[0]):
            row = PICK + 8 * s + k
            image = image + table_ref[row : row + 1, :] * img_ref[k, 0:rows, :].astype(f32)
        outs[s][...] = image.astype(bf16)


def pick(img, table, rows):
    shape = jax.ShapeDtypeStruct((rows, img.shape[2]), bf16)
    return pl.pallas_call(
        pick_kernel,
        in_specs=[VMEM, VMEM],
        out_specs=(VMEM,) * FRAMES,
        out_shape=(shape,) * FRAMES,
        compiler_params=pltpu.CompilerParams(vmem_limit_bytes=SMALL),
        name="pick",
    )(img, table)


def choose_kernel(table_ref, *refs):
    image = jnp.zeros(refs[0].shape, f32)
    for s in range(FRAMES):
        image = image + table_ref[FROM + s : FROM + s + 1, :] * refs[s][...].astype(f32)
    refs[FRAMES][...] = image


def choose(table, images):
    return pl.pallas_call(
        choose_kernel,
        in_specs=[VMEM] * (1 + FRAMES),
        out_specs=VMEM,
        out_shape=jax.ShapeDtypeStruct(images[0].shape, f32),
        compiler_params=pltpu.CompilerParams(vmem_limit_bytes=SMALL),
        name="choose",
    )(table, *images)


def update_kernel(img_ref, table_ref, flat_ref, vol_ref, out_hbm, obuf, osem):
    refl = img_ref.shape[0]
    ext, cells = vol_ref.shape
    rows, chunk = obuf.shape[1:]
    img = jnp.concatenate(
        [img_ref[k] * table_ref[MASK + k : MASK + k + 1, :].astype(bf16) for k in range(refl)], axis=1
    )
    scale = table_ref[SCALE : SCALE + 1, 0:1]
    place = lax.broadcasted_iota(jnp.int32, (ext, 1), 0)
    bound = jnp.where(
        place == rows - 1,
        table_ref[BOUND : BOUND + 1, 0:1],
        jnp.where(place == ext - 1, table_ref[BOUND + 1 : BOUND + 2, 0:1], huber_delta),
    )

    def out_copy(i, slot):
        at = pl.ds(pl.multiple_of(i * chunk, chunk), chunk)
        return pltpu.make_async_copy(obuf.at[slot], out_hbm.at[:, at], osem.at[slot])

    def step(i, carry):
        at = pl.ds(pl.multiple_of(i * chunk, chunk), chunk)
        slot = lax.rem(i, 2)
        gradient = lax.dot_general(
            img, flat_ref[at, :], (((1,), (1,)), ((), ())), preferred_element_type=f32
        )
        density = vol_ref[:, at].astype(f32) + scale * gradient
        for _ in range(SWEEPS):
            flux = pltpu.roll(density, ext - 1, 0) - density
            flux = jnp.minimum(jnp.maximum(flux, -bound), bound)
            density = density + sweep_rate * (flux - pltpu.roll(flux, 1, 0))

        @pl.when(i >= 2)
        def _():
            out_copy(i - 2, slot).wait()

        obuf[slot] = density[:rows].astype(bf16)
        out_copy(i, slot).start()
        return carry

    steps = cells // chunk
    lax.fori_loop(0, steps, step, 0)
    for i in range(steps - 2, steps):
        out_copy(i, i % 2).wait()


def update(img, table, flat, vol_ext, chunk=1024):
    ext, cells = vol_ext.shape
    rows = ext - HALO
    return pl.pallas_call(
        update_kernel,
        in_specs=[VMEM] * 4,
        out_specs=HBM,
        out_shape=jax.ShapeDtypeStruct((rows, cells), bf16),
        scratch_shapes=[pltpu.VMEM((2, rows, chunk), bf16), pltpu.SemaphoreType.DMA((2,))],
        compiler_params=pltpu.CompilerParams(vmem_limit_bytes=24 << 20),
        name="update",
    )(img, table, flat, vol_ext)


def local(volume, rays, band_start, band_len, slot_image, measured, relax):
    cells, refl, det = rays.shape
    rows = volume.shape[1]
    slabs = lax.axis_size("slab")
    orients = lax.axis_size("orient")
    members = orients // FRAMES
    classes = [[g * FRAMES + q for g in range(members)] for q in range(FRAMES)]
    vol = volume[0]
    meas = measured[0]
    step_gain = math.sqrt(cells * orients / (FRAMES * refl * det))

    low, high, meas, table = prepare(
        vol, band_start[:, 0], band_len[:, 0], slot_image, meas, relax, step_gain, slabs
    )

    above = lax.ppermute(low, "slab", [(i, i + 1) for i in range(slabs - 1)])
    below = lax.ppermute(high, "slab", [(i + 1, i) for i in range(slabs - 1)])
    meas_ext = extend(meas, below, above)

    swaps = [[(o, o ^ s) for o in range(orients)] for s in range(FRAMES)]
    gathered = [meas_ext] + [lax.ppermute(meas_ext, "orient", swaps[s]) for s in range(1, FRAMES)]

    proj, flat, vol_ext = project(vol, below, above, rays, table)

    part = combine(proj, table, gathered)
    pieces = lax.all_to_all(part, "orient", 0, 0, axis_index_groups=classes, tiled=True)
    images = lax.all_to_all(total(pieces), "orient", 0, 0, axis_index_groups=classes, tiled=True)

    picked = pick(images, table, rows)
    arrived = [picked[0]] + [lax.ppermute(picked[s], "orient", swaps[s]) for s in range(1, FRAMES)]
    updated = update(images, table, flat, vol_ext)
    residual = choose(table, arrived)
    return (updated[None], residual[None])


def solution(mesh):
    placed = (
        P("orient", "slab", None),
        P(),
        P(None, "orient"),
        P(None, "orient"),
        P(),
        P("orient", "slab", None),
        P("orient"),
    )
    return jax.shard_map(
        local,
        mesh=mesh,
        in_specs=placed,
        out_specs=(P("orient", "slab", None), P("orient", "slab", None)),
        check_vma=False,
    )
```

time: 91 us -> 69.1 us (0.76)
  local copies, waits for them, and re-layouts: 15.3 us -> 0 us
  blocking collectives: 16.7 us -> 28 us
  between operations: 12.2 us -> 1.38 us
  other arithmetic: 7.34 us -> 0 us
  starting transfers between devices: 17.6 us -> 11.6 us
  waiting for transfers between devices: 0.52 us -> 4.82 us
  Pallas kernels: 20.8 us -> 23 us
    unnamed x10 -> x0, local copies, waits for them, and re-layouts: 12.9 us -> none
    all_to_all x1 -> x2, blocking collectives: 16.7 us -> 28 us  [the longest x1 16.5 us: local(): lax.all_to_all(part, 'orient', 0, 0, axis_index_groups=classes, tiled=True)]
    convert_element_type x10 -> x0, other arithmetic: 4.84 us -> none  [the longest x2 2.65 us: local(): held = (wanted == slot_image[orient ^ s]).astype(f32)]
    ppermute x8, waiting for transfers between devices: 0.02 us -> 4.82 us  [the longest x1 4.8 us: local(): above = lax.ppermute(low, 'slab', [(i, i + 1) for i in range(slabs - 1)])]
    all_to_all x1 -> x0, starting transfers between devices: 3.42 us -> none  [local(): lax.all_to_all(jnp.broadcast_to(own[None], (members, rows + HALO, det)),...]
    ppermute x8, starting transfers between devices: 14.2 us -> 11.6 us  [the longest x3 3.57 us: local(): lax.ppermute(meas_ext, 'orient', swaps[s])]
    pallas_call x2 -> x8, Pallas kernels: 20.8 us -> 23 us  [the longest x1 11 us: update(): pl.pallas_call(update_kernel, in_specs=[VMEM] * 4, out_specs=HBM, out_sha...]
    dynamic_slice x1 -> x0, local copies, waits for them, and re-layouts: 1.47 us -> none  [local(): held = (wanted == slot_image[orient ^ s]).astype(f32)]
  transfers between devices with their start and end apart: 9 -> 8, of which waited for: 1 -> 1; matrix products, arithmetic and copies ran while one was open for 6% -> 0% of each run, Pallas kernels for 23% -> 30%
where the time goes in v2:
time: 69.1 us; the launch traced here: 68.9 us
  blocking collectives  28 us (41%)
  Pallas kernels  23 us (33%)
  starting transfers between devices  11.6 us (17%)
  waiting for transfers between devices  4.82 us (7%)
  between operations  1.38 us (2%)
    all_to_all x1, blocking collectives, local(): lax.all_to_all(part, 'orient', 0, 0, axis_index_groups=classes, tiled=True)  16.5 us
    all_to_all x1, blocking collectives, local(): lax.all_to_all(total(pieces), 'orient', 0, 0, axis_index_groups=classes,...  11.5 us
    pallas_call x1, Pallas kernels, update(): pl.pallas_call(update_kernel, in_specs=[VMEM] * 4, out_specs=HBM, out_sha...  11 us
    pallas_call x1, Pallas kernels, project(): pl.pallas_call(project_kernel, in_specs=[HBM, VMEM, VMEM, HBM, VMEM], out...  9.68 us
    ppermute x1, waiting for transfers between devices, local(): above = lax.ppermute(low, 'slab', [(i, i + 1) for i in range(slabs - 1)])  4.8 us
    ppermute x3, starting transfers between devices, local(): lax.ppermute(meas_ext, 'orient', swaps[s])  3.57 us
    ppermute x3, starting transfers between devices, local(): lax.ppermute(picked[s], 'orient', swaps[s])  3.57 us
    ppermute x1, starting transfers between devices, local(): below = lax.ppermute(high, 'slab', [(i + 1, i) for i in range(slabs - 1)])  2.58 us
  transfers between devices with their start and end apart: 8, of which 1 were waited for; matrix products, arithmetic and copies ran while one was open for 0% of the time, Pallas kernels for 30%

profile of v2, /device:TPU:24, one launch (start us, length us, event | category | flops | bytes accessed | tf_op | source)
XLA Modules:
  0.0 68.9 jit_solution(9065388388380429039)
XLA Ops:
  1.3 1.2 %prepare.1 = (bf16[2,8320]{1,0:T(2,128)(2,1)S(1)}, bf16[2,8320]{1,0:T(2,128)(2,1)S(1)}, f32[128,128]{1,0:T(8,128)S(1)}, f32[80,128]{1,0:T(8,128)S(1)}) custom-call(bf16[128,8192]{1,0:T(8,128)(2,1)} %bitcast.6, f32[128,128]{1,0:T(8,128)} %bitcast.9, s32[8]{0:T(128)} %bitcast.11, s32[8]{0:T(128)} %bitcast.12, s32[32]{0:T(128)} %refs_4_.1, f32[1]{0:T(128)S(6)} %copy.9.refs_5_), custom_call_target="tpu_custom_call" | custom-call | tf_op jit(solution)/shard_map/prepare/pallas_call | solution.py:95
  2.5 2.6 %collective-permute-start = (bf16[2,8320]{1,0:T(2,128)(2,1)S(1)}, bf16[2,8320]{1,0:T(2,128)(2,1)S(1)}, u32[]{:S(2)}, u32[]{:S(2)}) collective-permute-start(bf16[2,8320]{1,0:T(2,128)(2,1)S(1)} %get-tuple-element.13), channel_id=1, source_target_pairs={{1,0},{2,1},{3,2},{5,4},{6,5},{7,6},{9,8},{10,9},{11,10},{13,12},{... | collective-permute-start | bytes 99848 | tf_op jit(solution)/shard_map/ppermute | solution.py:354
  5.1 1.9 %collective-permute-start.1 = (bf16[2,8320]{1,0:T(2,128)(2,1)S(1)}, bf16[2,8320]{1,0:T(2,128)(2,1)S(1)}, u32[]{:S(2)}, u32[]{:S(2)}) collective-permute-start(bf16[2,8320]{1,0:T(2,128)(2,1)S(1)} %get-tuple-element.14), channel_id=1, source_target_pairs={{0,1},{1,2},{2,3},{4,5},{5,6},{6,7},{8,9},{9,10},{10,11},{12,13},{... | collective-permute-start | bytes 99848 | tf_op jit(solution)/shard_map/ppermute | solution.py:353
  7.0 0.0 collective-permute-done.below_ref
  7.0 4.8 %collective-permute-done.1.above_ref = bf16[2,8320]{1,0:T(2,128)(2,1)S(1)} collective-permute-done((bf16[2,8320]{1,0:T(2,128)(2,1)S(1)}, bf16[2,8320]{1,0:T(2,128)(2,1)S(1)}, u32[]{:S(2)}, u32[]{:S(2)}) %collective-permute-start.1) | collective-permute-done | bytes 33312 | tf_op jit(solution)/shard_map/ppermute | solution.py:353
  11.8 1.9 %collective-permute-start.4 = (bf16[144,128]{1,0:T(8,128)(2,1)S(1)}, bf16[144,128]{1,0:T(8,128)(2,1)S(1)}, u32[]{:S(2)}, u32[]{:S(2)}) collective-permute-start(bf16[144,128]{1,0:T(8,128)(2,1)S(1)} %extend.1.refs_0_), channel_id=1, source_target_pairs={{0,12},{4,8},{8,4},{12,0},{16,28},{20,24},{24,20},{28,16},{32,44},... | collective-permute-start | bytes 110600 | tf_op jit(solution)/shard_map/ppermute | solution.py:358
  13.7 0.2 collective-permute-start.3
  13.9 1.5 %collective-permute-start.2 = (bf16[144,128]{1,0:T(8,128)(2,1)S(1)}, bf16[144,128]{1,0:T(8,128)(2,1)S(1)}, u32[]{:S(2)}, u32[]{:S(2)}) collective-permute-start(bf16[144,128]{1,0:T(8,128)(2,1)S(1)} %extend.1.refs_0_), channel_id=1, source_target_pairs={{0,4},{4,0},{8,12},{12,8},{16,20},{20,16},{24,28},{28,24},{32,36},... | collective-permute-start | bytes 110600 | tf_op jit(solution)/shard_map/ppermute | solution.py:358
  15.4 9.7 %project.1 = (f32[8,144,128]{2,1,0:T(8,128)S(1)}, bf16[8192,1024]{1,0:T(8,128)(2,1)S(1)}, bf16[144,8192]{1,0:T(8,128)(2,1)S(1)}) custom-call(bf16[128,8192]{1,0:T(8,128)(2,1)} %bitcast.7, bf16[2,8320]{1,0:T(2,128)(2,1)S(1)} %collective-permute-done.below_ref, bf16[2,8320]{1,0:T(2,128)(2,1)S(1)} %collective-permute-done.1.above_ref, ...), custom_call_target="tpu_custom_call" | custom-call | tf_op jit(solution)/shard_map/project/pallas_call | solution.py:176
  25.1 0.0 collective-permute-done.4.refs_3_
  25.1 0.0 collective-permute-done.3.refs_2_
  25.1 0.0 collective-permute-done.2.refs_1_
  25.1 0.2 combine.1
  25.3 16.5 %all_to_all.10.pieces_ref = bf16[8,144,128]{2,1,0:T(8,128)(2,1)S(1)} all-to-all(bf16[8,144,128]{2,1,0:T(8,128)(2,1)S(1)} %combine.1), channel_id=1, replica_groups={{0,16,32,48,64,80,96,112},{4,20,36,52,68,84,100,116},{8,24,40,56,72,88,..., dimensions={0} | all-to-all | bytes 589824 | tf_op jit(solution)/shard_map/all_to_all | solution.py:363
  41.9 11.5 %all_to_all.11.img_ref = bf16[8,144,128]{2,1,0:T(8,128)(2,1)S(1)} all-to-all(bf16[8,144,128]{2,1,0:T(8,128)(2,1)S(1)} %total.1), channel_id=1, replica_groups={{0,16,32,48,64,80,96,112},{4,20,36,52,68,84,100,116},{8,24,40,56,72,88,..., dimensions={0} | all-to-all | bytes 589824 | tf_op jit(solution)/shard_map/all_to_all | solution.py:364
  53.4 0.2 pick.1
  53.6 0.3 collective-permute-start.5
  53.9 1.0 %collective-permute-start.6 = (bf16[128,128]{1,0:T(8,128)(2,1)S(1)}, bf16[128,128]{1,0:T(8,128)(2,1)S(1)}, u32[]{:S(2)}, u32[]{:S(2)}) collective-permute-start(bf16[128,128]{1,0:T(8,128)(2,1)S(1)} %get-tuple-element.22), channel_id=1, source_target_pairs={{0,8},{4,12},{8,0},{12,4},{16,24},{20,28},{24,16},{28,20},{32,40},... | collective-permute-start | bytes 98312 | tf_op jit(solution)/shard_map/ppermute | solution.py:367
  54.9 2.3 %collective-permute-start.7 = (bf16[128,128]{1,0:T(8,128)(2,1)S(1)}, bf16[128,128]{1,0:T(8,128)(2,1)S(1)}, u32[]{:S(2)}, u32[]{:S(2)}) collective-permute-start(bf16[128,128]{1,0:T(8,128)(2,1)S(1)} %get-tuple-element.23), channel_id=1, source_target_pairs={{0,12},{4,8},{8,4},{12,0},{16,28},{20,24},{24,20},{28,16},{32,44},... | collective-permute-start | bytes 98312 | tf_op jit(solution)/shard_map/ppermute | solution.py:367
  57.2 11.0 %update.1 = bf16[128,8192]{1,0:T(8,128)(2,1)} custom-call(bf16[8,144,128]{2,1,0:T(8,128)(2,1)S(1)} %all_to_all.11.img_ref, f32[80,128]{1,0:T(8,128)S(1)} %get-tuple-element.15.table_ref, bf16[8192,1024]{1,0:T(8,128)(2,1)S(1)} %get-tuple-element.18.flat_ref, bf16[144,8192]{1,0:T(8,128)(2,1)S(1)} %get-tuple-element.19.vol_ref), custom_call_target="tpu_custom_call" | custom-call | tf_op jit(solution)/shard_map/update/pallas_call | solution.py:327
  68.2 0.0 collective-permute-done.5.refs_1_
  68.2 0.0 collective-permute-done.6.refs_2_
  68.2 0.0 collective-permute-done.7.refs_3_
  68.2 0.7 choose.1
  (2 shorter events, 0.1 us)
Async XLA Ops:
  2.5 4.5 %collective-permute-start = (bf16[2,8320]{1,0:T(2,128)(2,1)S(1)}, bf16[2,8320]{1,0:T(2,128)(2,1)S(1)}, u32[]{:S(2)}, u32[]{:S(2)}) collective-permute-start(bf16[2,8320]{1,0:T(2,128)(2,1)S(1)} %get-tuple-element.13), channel_id=1, source_target_pairs={{1,0},{2,1},{3,2},{5,4},{6,5},{7,6},{9,8},{10,9},{11,10},{13,12},{... | collective-permute-start | bytes 99848 | tf_op jit(solution)/shard_map/ppermute | solution.py:354
  5.1 6.7 %collective-permute-start.1 = (bf16[2,8320]{1,0:T(2,128)(2,1)S(1)}, bf16[2,8320]{1,0:T(2,128)(2,1)S(1)}, u32[]{:S(2)}, u32[]{:S(2)}) collective-permute-start(bf16[2,8320]{1,0:T(2,128)(2,1)S(1)} %get-tuple-element.14), channel_id=1, source_target_pairs={{0,1},{1,2},{2,3},{4,5},{5,6},{6,7},{8,9},{9,10},{10,11},{12,13},{... | collective-permute-start | bytes 99848 | tf_op jit(solution)/shard_map/ppermute | solution.py:353
  11.8 13.3 %collective-permute-start.4 = (bf16[144,128]{1,0:T(8,128)(2,1)S(1)}, bf16[144,128]{1,0:T(8,128)(2,1)S(1)}, u32[]{:S(2)}, u32[]{:S(2)}) collective-permute-start(bf16[144,128]{1,0:T(8,128)(2,1)S(1)} %extend.1.refs_0_), channel_id=1, source_target_pairs={{0,12},{4,8},{8,4},{12,0},{16,28},{20,24},{24,20},{28,16},{32,44},... | collective-permute-start | bytes 110600 | tf_op jit(solution)/shard_map/ppermute | solution.py:358
  13.7 11.4 %collective-permute-start.3 = (bf16[144,128]{1,0:T(8,128)(2,1)S(1)}, bf16[144,128]{1,0:T(8,128)(2,1)S(1)}, u32[]{:S(2)}, u32[]{:S(2)}) collective-permute-start(bf16[144,128]{1,0:T(8,128)(2,1)S(1)} %extend.1.refs_0_), channel_id=1, source_target_pairs={{0,8},{4,12},{8,0},{12,4},{16,24},{20,28},{24,16},{28,20},{32,40},... | collective-permute-start | bytes 110600 | tf_op jit(solution)/shard_map/ppermute | solution.py:358
  13.9 11.2 %collective-permute-start.2 = (bf16[144,128]{1,0:T(8,128)(2,1)S(1)}, bf16[144,128]{1,0:T(8,128)(2,1)S(1)}, u32[]{:S(2)}, u32[]{:S(2)}) collective-permute-start(bf16[144,128]{1,0:T(8,128)(2,1)S(1)} %extend.1.refs_0_), channel_id=1, source_target_pairs={{0,4},{4,0},{8,12},{12,8},{16,20},{20,16},{24,28},{28,24},{32,36},... | collective-permute-start | bytes 110600 | tf_op jit(solution)/shard_map/ppermute | solution.py:358
  53.6 14.6 %collective-permute-start.5 = (bf16[128,128]{1,0:T(8,128)(2,1)S(1)}, bf16[128,128]{1,0:T(8,128)(2,1)S(1)}, u32[]{:S(2)}, u32[]{:S(2)}) collective-permute-start(bf16[128,128]{1,0:T(8,128)(2,1)S(1)} %get-tuple-element.21), channel_id=1, source_target_pairs={{0,4},{4,0},{8,12},{12,8},{16,20},{20,16},{24,28},{28,24},{32,36},... | collective-permute-start | bytes 98312 | tf_op jit(solution)/shard_map/ppermute | solution.py:367
  53.9 14.3 %collective-permute-start.6 = (bf16[128,128]{1,0:T(8,128)(2,1)S(1)}, bf16[128,128]{1,0:T(8,128)(2,1)S(1)}, u32[]{:S(2)}, u32[]{:S(2)}) collective-permute-start(bf16[128,128]{1,0:T(8,128)(2,1)S(1)} %get-tuple-element.22), channel_id=1, source_target_pairs={{0,8},{4,12},{8,0},{12,4},{16,24},{20,28},{24,16},{28,20},{32,40},... | collective-permute-start | bytes 98312 | tf_op jit(solution)/shard_map/ppermute | solution.py:367
  54.9 13.3 %collective-permute-start.7 = (bf16[128,128]{1,0:T(8,128)(2,1)S(1)}, bf16[128,128]{1,0:T(8,128)(2,1)S(1)}, u32[]{:S(2)}, u32[]{:S(2)}) collective-permute-start(bf16[128,128]{1,0:T(8,128)(2,1)S(1)} %get-tuple-element.23), channel_id=1, source_target_pairs={{0,12},{4,8},{8,4},{12,0},{16,28},{20,24},{24,20},{28,16},{32,44},... | collective-permute-start | bytes 98312 | tf_op jit(solution)/shard_map/ppermute | solution.py:367

commit v3 on v2

--- a/solution.py
+++ b/solution.py
@@ -18,6 +18,7 @@
 f32 = jnp.float32
 
 
+PIECE = 64
 SMALL = 4 << 20
 
 MASK = 0
@@ -38,7 +39,7 @@
 
 
 def prepare_kernel(step_gain, slabs, vol_hbm, meas_hbm, start_hbm, len_hbm, slot_hbm, relax_ref,
-                   low_ref, high_ref, meas_ref, table_ref,
+                   near_ref, far_ref, meas_ref, table_ref,
                    first, last, start_ref, len_ref, slot_ref, sem):
     rows, cells = vol_hbm.shape
     det = meas_ref.shape[1]
@@ -82,10 +83,19 @@
     table_ref[BOUND : BOUND + 1, :] = line(slab != slabs - 1) * huber_delta
     table_ref[BOUND + 1 : BOUND + 2, :] = line(slab != 0) * huber_delta
     table_ref[BOUND + 2 : BOUND + 3, :] = line(slab < 0)
-    low_ref[:, cells:] = meas_ref[rows - 2 :, :].astype(bf16)
-    high_ref[:, cells:] = meas_ref[0:2, :].astype(bf16)
-    high_ref[:, 0:cells] = first[0:2, :]
-    low_ref[:, 0:cells] = last[tile - 2 :, :]
+    low = jnp.concatenate([last[tile - 2 :, :], meas_ref[rows - 2 :, :].astype(bf16)], axis=1)
+    high = jnp.concatenate([first[0:2, :], meas_ref[0:2, :].astype(bf16)], axis=1)
+    even = jnp.bitwise_and(slab, 1) == 0
+
+    @pl.when(even)
+    def _():
+        near_ref[...] = low
+        far_ref[...] = high
+
+    @pl.when(jnp.logical_not(even))
+    def _():
+        near_ref[...] = high
+        far_ref[...] = low
 
 
 def prepare(vol, start, length, slot_image, meas, relax, step_gain, slabs):
@@ -112,16 +122,22 @@
     )(*(keep(x) for x in (vol, meas, start, length, slot_image)), relax)
 
 
-def extend_kernel(meas_ref, below_ref, above_ref, ext_ref):
+def halo_rows(near, far, even):
+    below = jnp.where(even, near, far)
+    above = jnp.where(even, far, near)
+    zeros = jnp.zeros((HALO - 4, near.shape[1]), bf16)
+    return jnp.concatenate([below, zeros, above], axis=0)
+
+
+def extend_kernel(meas_ref, near_ref, far_ref, ext_ref):
     rows, det = meas_ref.shape
-    cells = below_ref.shape[1] - det
+    cells = near_ref.shape[1] - det
+    even = jnp.bitwise_and(lax.axis_index("slab"), 1) == 0
     ext_ref[0:rows] = meas_ref[...].astype(bf16)
-    ext_ref[rows:] = jnp.concatenate(
-        [below_ref[:, cells:], jnp.zeros((HALO - 4, det), bf16), above_ref[:, cells:]], axis=0
-    )
-
-
-def extend(meas, below, above):
+    ext_ref[rows:] = halo_rows(near_ref[:, cells:], far_ref[:, cells:], even)
+
+
+def extend(meas, near, far):
     rows, det = meas.shape
     return pl.pallas_call(
         extend_kernel,
@@ -130,46 +146,42 @@
         out_shape=jax.ShapeDtypeStruct((rows + HALO, det), bf16),
         compiler_params=pltpu.CompilerParams(vmem_limit_bytes=SMALL),
         name="extend",
-    )(meas, below, above)
-
-
-def project_kernel(vol_hbm, below_ref, above_ref, rays_hbm, table_ref, proj_ref, flat_ref, vol_ref, buf, acc, vsem, rsem):
+    )(meas, near, far)
+
+
+def project_kernel(vol_hbm, near_ref, far_ref, rays_hbm, table_ref, proj_ref, flat_ref, vol_ref, buf, acc, vsem, rsem):
     chunks = rsem.shape[0]
-    chunk = buf.shape[0] // chunks
     rows, cells = vol_hbm.shape
-    refl, det = rays_hbm.shape[1:]
-
-    def rays_copy(i):
-        at = pl.ds(pl.multiple_of(i * chunk, chunk), chunk)
-        return pltpu.make_async_copy(rays_hbm.at[at], buf.at[at], rsem.at[i])
-
-    def vol_copy(i):
-        at = pl.ds(pl.multiple_of(i * chunk, chunk), chunk)
-        return pltpu.make_async_copy(vol_hbm.at[:, at], vol_ref.at[0:rows, at], vsem.at[i])
+    chunk = cells // chunks
+    refl = buf.shape[0] // cells
+    det = buf.shape[1]
+
+    def copies(i):
+        at = slice(i * chunk, (i + 1) * chunk)
+        wide = slice(i * chunk * refl, (i + 1) * chunk * refl)
+        return (
+            pltpu.make_async_copy(vol_hbm.at[:, at], vol_ref.at[0:rows, at], vsem.at[i]),
+            pltpu.make_async_copy(rays_hbm.at[wide], buf.at[wide], rsem.at[i]),
+        )
 
     for i in range(chunks):
-        vol_copy(i).start()
-        rays_copy(i).start()
-    vol_ref[rows:, :] = jnp.concatenate(
-        [below_ref[:, 0:cells], jnp.zeros((HALO - 4, cells), bf16), above_ref[:, 0:cells]], axis=0
-    )
-    acc[...] = jnp.zeros_like(acc)
-
-    def step(i, carry):
-        at = pl.ds(pl.multiple_of(i * chunk, chunk), chunk)
-        vol_copy(i).wait()
-        rays_copy(i).wait()
-        flat = buf[at].reshape(chunk, refl * det)
-        flat_ref[at, :] = flat
-        acc[...] += jnp.dot(vol_ref[:, at], flat, preferred_element_type=f32)
-        return carry
-
-    lax.fori_loop(0, chunks, step, 0)
+        for copy in copies(i):
+            copy.start()
+    even = jnp.bitwise_and(lax.axis_index("slab"), 1) == 0
+    vol_ref[rows:, :] = halo_rows(near_ref[:, 0:cells], far_ref[:, 0:cells], even)
+    for i in range(chunks):
+        for copy in copies(i):
+            copy.wait()
+        at = slice(i * chunk, (i + 1) * chunk)
+        for j in range(i * chunk, (i + 1) * chunk, PIECE):
+            flat_ref[j : j + PIECE, :] = buf[j * refl : (j + PIECE) * refl].reshape(PIECE, refl * det)
+        part = jnp.dot(vol_ref[:, at], flat_ref[at, :], preferred_element_type=f32)
+        acc[...] = part if i == 0 else acc[...] + part
     for k in range(refl):
         proj_ref[k] = acc[:, k * det : (k + 1) * det] * table_ref[MASK + k : MASK + k + 1, :]
 
 
-def project(vol, below, above, rays, table, chunk=1024):
+def project(vol, near, far, rays, table, chunk=1024):
     rows, cells = vol.shape
     refl, det = rays.shape[1:]
     ext = rows + HALO
@@ -183,14 +195,52 @@
             pltpu.VMEM((ext, cells), bf16),
         ),
         scratch_shapes=[
-            pltpu.VMEM(rays.shape, bf16),
+            pltpu.VMEM((cells * refl, det), bf16),
             pltpu.VMEM((ext, refl * det), f32),
             pltpu.SemaphoreType.DMA((cells // chunk,)),
             pltpu.SemaphoreType.DMA((cells // chunk,)),
         ],
         compiler_params=pltpu.CompilerParams(vmem_limit_bytes=24 << 20),
         name="project",
-    )(keep(vol), below, above, keep(rays), table)
+    )(keep(vol), near, far, keep(rays.reshape(cells * refl, det)), table)
+
+
+def fold_kernel(flat_ref, table_ref, out_ref):
+    cells, wide = flat_ref.shape
+    det = table_ref.shape[1]
+    low = lax.broadcasted_iota(jnp.int32, (1, det), 1) < det // 2
+    low_block = jnp.broadcast_to(low, (PIECE, det))
+    keeps = []
+    for p in range(wide // (2 * det)):
+        k = MASK + 2 * p
+        line = jnp.where(low, table_ref[k : k + 1, :], table_ref[k + 1 : k + 2, :])
+        keeps.append(jnp.broadcast_to(line.astype(bf16), (PIECE, det)) > 0.5)
+
+    def step(i, carry):
+        at = pl.ds(pl.multiple_of(i * PIECE, PIECE), PIECE)
+        for p, stay in enumerate(keeps):
+            first = flat_ref[at, 2 * p * det : (2 * p + 1) * det]
+            second = flat_ref[at, (2 * p + 1) * det : (2 * p + 2) * det]
+            straight = jnp.where(low_block, first, second)
+            crossed = jnp.where(low_block, second, first)
+            out_ref[at, p * det : (p + 1) * det] = jnp.where(
+                stay, straight, pltpu.roll(crossed, det // 2, 1)
+            )
+        return carry
+
+    lax.fori_loop(0, cells // PIECE, step, 0)
+
+
+def fold(flat, table):
+    cells, wide = flat.shape
+    return pl.pallas_call(
+        fold_kernel,
+        in_specs=[VMEM, VMEM],
+        out_specs=VMEM,
+        out_shape=pltpu.VMEM((cells, wide // 2), bf16),
+        compiler_params=pltpu.CompilerParams(vmem_limit_bytes=SMALL),
+        name="fold",
+    )(flat, table)
 
 
 def combine_kernel(proj_ref, table_ref, *refs):
@@ -276,61 +326,95 @@
     )(table, *images)
 
 
-def update_kernel(img_ref, table_ref, flat_ref, vol_ref, out_hbm, obuf, osem):
-    refl = img_ref.shape[0]
-    ext, cells = vol_ref.shape
-    rows, chunk = obuf.shape[1:]
-    img = jnp.concatenate(
-        [img_ref[k] * table_ref[MASK + k : MASK + k + 1, :].astype(bf16) for k in range(refl)], axis=1
+def update_kernel(img_ref, table_ref, flat_ref, vol_ref, out_hbm, dbuf, fbuf, obuf, osem):
+    refl, ext, det = img_ref.shape
+    cells = vol_ref.shape[1]
+    rows = ext - HALO
+    slots = dbuf.shape[0]
+    tiles = slots // 2
+    chunk = tiles * det
+    steps = cells // chunk
+    sends = osem.shape[0]
+
+    low = lax.broadcasted_iota(jnp.int32, (1, det), 1) < det // 2
+    parts = []
+    for k in range(0, refl, 2):
+        first = img_ref[k].astype(f32) * table_ref[MASK + k : MASK + k + 1, :]
+        second = img_ref[k + 1].astype(f32) * table_ref[MASK + k + 1 : MASK + k + 2, :]
+        straight = jnp.where(low, first, second)
+        crossed = jnp.where(low, second, first)
+        parts.append((straight + pltpu.roll(crossed, det // 2, 1)).astype(bf16))
+    img = jnp.concatenate(parts, axis=1)
+    scale = table_ref[SCALE : SCALE + 1, 0:1]
+
+    place = lax.broadcasted_iota(jnp.int32, (ext, det), 0)
+    bound = jnp.where(
+        place == rows + 7,
+        table_ref[BOUND : BOUND + 1, :],
+        jnp.where(place == 7, table_ref[BOUND + 1 : BOUND + 2, :], huber_delta),
     )
-    scale = table_ref[SCALE : SCALE + 1, 0:1]
-    place = lax.broadcasted_iota(jnp.int32, (ext, 1), 0)
-    bound = jnp.where(
-        place == rows - 1,
-        table_ref[BOUND : BOUND + 1, 0:1],
-        jnp.where(place == ext - 1, table_ref[BOUND + 1 : BOUND + 2, 0:1], huber_delta),
-    )
-
-    def out_copy(i, slot):
-        at = pl.ds(pl.multiple_of(i * chunk, chunk), chunk)
-        return pltpu.make_async_copy(obuf.at[slot], out_hbm.at[:, at], osem.at[slot])
-
-    def step(i, carry):
-        at = pl.ds(pl.multiple_of(i * chunk, chunk), chunk)
-        slot = lax.rem(i, 2)
+    zeros = jnp.zeros((8, det), f32)
+    for q in range(slots):
+        dbuf[q, 0:8] = zeros
+        dbuf[q, 8 + ext :] = zeros
+        fbuf[q, 0:8] = zeros
+
+    def psi(t, first):
+        limit = bound[first : first + t.shape[0]]
+        return jnp.minimum(jnp.maximum(t, -limit), limit)
+
+    def backproject(i):
+        at = slice(i * chunk, (i + 1) * chunk)
         gradient = lax.dot_general(
             img, flat_ref[at, :], (((1,), (1,)), ((), ())), preferred_element_type=f32
         )
         density = vol_ref[:, at].astype(f32) + scale * gradient
-        for _ in range(SWEEPS):
-            flux = pltpu.roll(density, ext - 1, 0) - density
-            flux = jnp.minimum(jnp.maximum(flux, -bound), bound)
-            density = density + sweep_rate * (flux - pltpu.roll(flux, 1, 0))
-
-        @pl.when(i >= 2)
-        def _():
-            out_copy(i - 2, slot).wait()
-
-        obuf[slot] = density[:rows].astype(bf16)
-        out_copy(i, slot).start()
-        return carry
-
-    steps = cells // chunk
-    lax.fori_loop(0, steps, step, 0)
-    for i in range(steps - 2, steps):
-        out_copy(i, i % 2).wait()
-
-
-def update(img, table, flat, vol_ext, chunk=1024):
+        for t in range(tiles):
+            q = (i * tiles + t) % slots
+            lanes = slice(t * det, (t + 1) * det)
+            dbuf[q, 8:16] = density[ext - 8 :, lanes]
+            dbuf[q, 16 : 8 + ext] = density[0 : ext - 8, lanes]
+
+    def out_copy(j):
+        at = slice(j * (cells // sends), (j + 1) * (cells // sends))
+        return pltpu.make_async_copy(obuf.at[:, at], out_hbm.at[:, at], osem.at[j])
+
+    def smooth(i):
+        for t in range(tiles):
+            q = (i * tiles + t) % slots
+            here = dbuf[q, 8 : 8 + ext]
+            flux = psi(dbuf[q, 9 : 9 + ext] - here, 0)
+            fbuf[q, 8 : 8 + ext] = flux
+            once = here + sweep_rate * (flux - fbuf[q, 7 : 7 + ext])
+            dbuf[q, 8 : 8 + ext] = once
+            fbuf[q, 8 : 16 + rows] = psi(dbuf[q, 9 : 17 + rows] - once[0 : 8 + rows], 0)
+            net = fbuf[q, 16 : 16 + rows] - fbuf[q, 15 : 15 + rows]
+            at = slice(i * chunk + t * det, i * chunk + (t + 1) * det)
+            obuf[:, at] = (once[8 : 8 + rows] + sweep_rate * net).astype(bf16)
+        if (i + 1) * sends % steps == 0:
+            out_copy((i + 1) * sends // steps - 1).start()
+
+    backproject(0)
+    for i in range(1, steps):
+        backproject(i)
+        smooth(i - 1)
+    smooth(steps - 1)
+    for j in range(sends):
+        out_copy(j).wait()
+
+
+def update(img, table, flat, vol_ext, chunk=256, sends=8):
     ext, cells = vol_ext.shape
     rows = ext - HALO
+    det = img.shape[2]
+    slot = pltpu.VMEM((2 * chunk // det, ext + 16, det), f32)
     return pl.pallas_call(
         update_kernel,
         in_specs=[VMEM] * 4,
         out_specs=HBM,
         out_shape=jax.ShapeDtypeStruct((rows, cells), bf16),
-        scratch_shapes=[pltpu.VMEM((2, rows, chunk), bf16), pltpu.SemaphoreType.DMA((2,))],
-        compiler_params=pltpu.CompilerParams(vmem_limit_bytes=24 << 20),
+        scratch_shapes=[slot, slot, pltpu.VMEM((rows, cells), bf16), pltpu.SemaphoreType.DMA((sends,))],
+        compiler_params=pltpu.CompilerParams(vmem_limit_bytes=8 << 20),
         name="update",
     )(img, table, flat, vol_ext)
 
@@ -346,18 +430,19 @@
     meas = measured[0]
     step_gain = math.sqrt(cells * orients / (FRAMES * refl * det))
 
-    low, high, meas, table = prepare(
+    near, far, meas, table = prepare(
         vol, band_start[:, 0], band_len[:, 0], slot_image, meas, relax, step_gain, slabs
     )
 
-    above = lax.ppermute(low, "slab", [(i, i + 1) for i in range(slabs - 1)])
-    below = lax.ppermute(high, "slab", [(i + 1, i) for i in range(slabs - 1)])
-    meas_ext = extend(meas, below, above)
+    near = lax.ppermute(near, "slab", [(i, i ^ 1) for i in range(slabs)])
+    far = lax.ppermute(far, "slab", [(i, slabs - 1 - i) for i in range(slabs)])
+    meas_ext = extend(meas, near, far)
 
     swaps = [[(o, o ^ s) for o in range(orients)] for s in range(FRAMES)]
     gathered = [meas_ext] + [lax.ppermute(meas_ext, "orient", swaps[s]) for s in range(1, FRAMES)]
 
-    proj, flat, vol_ext = project(vol, below, above, rays, table)
+    proj, flat, vol_ext = project(vol, near, far, rays, table)
+    flat = fold(flat, table)
 
     part = combine(proj, table, gathered)
     pieces = lax.all_to_all(part, "orient", 0, 0, axis_index_groups=classes, tiled=True)

time: 69.1 us -> 70.1 us (1.014)
  Pallas kernels: 23 us -> 28.1 us
  starting transfers between devices: 11.6 us -> 8.56 us
  waiting for transfers between devices: 4.82 us -> 3.61 us
    pallas_call x0 -> x1, Pallas kernels: none -> 11.3 us  [fold(): pl.pallas_call(fold_kernel, in_specs=[VMEM, VMEM], out_specs=VMEM, out_sh...]
    pallas_call x1, Pallas kernels: 11 us -> 5 us  [update(): pl.pallas_call(update_kernel, in_specs=[VMEM] * 4, out_specs=HBM, out_sha...]
    ppermute x2, starting transfers between devices: 4.5 us -> 1.42 us  [the longest x1 1.34 us: local(): far = lax.ppermute(far, 'slab', [(i, slabs - 1 - i) for i in range(slabs)])]
    ppermute x2, waiting for transfers between devices: 4.81 us -> 3.59 us  [the longest x1 3.59 us: local(): far = lax.ppermute(far, 'slab', [(i, slabs - 1 - i) for i in range(slabs)])]
  transfers between devices with their start and end apart: 8 -> 8, of which waited for: 1 -> 1; matrix products, arithmetic and copies ran while one was open for 0% -> 0% of each run, Pallas kernels for 30% -> 37%
where the time goes in v3:
time: 70.1 us; the launch traced here: 69.7 us
  Pallas kernels  28.1 us (40%)
  blocking collectives  28 us (40%)
  starting transfers between devices  8.56 us (12%)
  waiting for transfers between devices  3.61 us (5%)
  between operations  1.38 us (2%)
    all_to_all x1, blocking collectives, local(): lax.all_to_all(part, 'orient', 0, 0, axis_index_groups=classes, tiled=True)  16.5 us
    all_to_all x1, blocking collectives, local(): lax.all_to_all(total(pieces), 'orient', 0, 0, axis_index_groups=classes,...  11.5 us
    pallas_call x1, Pallas kernels, fold(): pl.pallas_call(fold_kernel, in_specs=[VMEM, VMEM], out_specs=VMEM, out_sh...  11.3 us
    pallas_call x1, Pallas kernels, project(): pl.pallas_call(project_kernel, in_specs=[HBM, VMEM, VMEM, HBM, VMEM], out...  9.49 us
    pallas_call x1, Pallas kernels, update(): pl.pallas_call(update_kernel, in_specs=[VMEM] * 4, out_specs=HBM, out_sha...  5 us
    ppermute x1, waiting for transfers between devices, local(): far = lax.ppermute(far, 'slab', [(i, slabs - 1 - i) for i in range(slabs)])  3.59 us
    ppermute x3, starting transfers between devices, local(): lax.ppermute(picked[s], 'orient', swaps[s])  3.57 us
    ppermute x3, starting transfers between devices, local(): lax.ppermute(meas_ext, 'orient', swaps[s])  3.57 us
  transfers between devices with their start and end apart: 8, of which 1 were waited for; matrix products, arithmetic and copies ran while one was open for 0% of the time, Pallas kernels for 37%

profile of v3, /device:TPU:24, one launch (start us, length us, event | category | flops | bytes accessed | tf_op | source)
XLA Modules:
  0.0 69.7 jit_solution(10868446920191669488)
XLA Ops:
  1.3 1.2 %prepare.1 = (bf16[2,8320]{1,0:T(2,128)(2,1)S(1)}, bf16[2,8320]{1,0:T(2,128)(2,1)S(1)}, f32[128,128]{1,0:T(8,128)S(1)}, f32[80,128]{1,0:T(8,128)S(1)}) custom-call(bf16[128,8192]{1,0:T(8,128)(2,1)} %bitcast.8, f32[128,128]{1,0:T(8,128)} %bitcast.11, s32[8]{0:T(128)} %bitcast.13, s32[8]{0:T(128)} %bitcast.14, s32[32]{0:T(128)} %refs_4_.1, f32[1]{0:T(128)S(6)} %copy.9.refs_5_), custom_call_target="tpu_custom_call" | custom-call | tf_op jit(solution)/shard_map/prepare/pallas_call | solution.py:105
  2.5 0.1 collective-permute-start
  2.6 1.3 %collective-permute-start.1 = (bf16[2,8320]{1,0:T(2,128)(2,1)S(1)}, bf16[2,8320]{1,0:T(2,128)(2,1)S(1)}, u32[]{:S(2)}, u32[]{:S(2)}) collective-permute-start(bf16[2,8320]{1,0:T(2,128)(2,1)S(1)} %get-tuple-element.14), channel_id=1, source_target_pairs={{0,3},{1,2},{2,1},{3,0},{4,7},{5,6},{6,5},{7,4},{8,11},{9,10},{10,... | collective-permute-start | bytes 99848 | tf_op jit(solution)/shard_map/ppermute | solution.py:438
  3.9 0.0 collective-permute-done.near_ref
  3.9 3.6 %collective-permute-done.1.far_ref = bf16[2,8320]{1,0:T(2,128)(2,1)S(1)} collective-permute-done((bf16[2,8320]{1,0:T(2,128)(2,1)S(1)}, bf16[2,8320]{1,0:T(2,128)(2,1)S(1)}, u32[]{:S(2)}, u32[]{:S(2)}) %collective-permute-start.1) | collective-permute-done | bytes 33312 | tf_op jit(solution)/shard_map/ppermute | solution.py:438
  7.6 0.8 %collective-permute-start.2 = (bf16[144,128]{1,0:T(8,128)(2,1)S(1)}, bf16[144,128]{1,0:T(8,128)(2,1)S(1)}, u32[]{:S(2)}, u32[]{:S(2)}) collective-permute-start(bf16[144,128]{1,0:T(8,128)(2,1)S(1)} %extend.1.refs_0_), channel_id=1, source_target_pairs={{0,4},{4,0},{8,12},{12,8},{16,20},{20,16},{24,28},{28,24},{32,36},... | collective-permute-start | bytes 110600 | tf_op jit(solution)/shard_map/ppermute | solution.py:442
  8.4 1.9 %collective-permute-start.3 = (bf16[144,128]{1,0:T(8,128)(2,1)S(1)}, bf16[144,128]{1,0:T(8,128)(2,1)S(1)}, u32[]{:S(2)}, u32[]{:S(2)}) collective-permute-start(bf16[144,128]{1,0:T(8,128)(2,1)S(1)} %extend.1.refs_0_), channel_id=1, source_target_pairs={{0,8},{4,12},{8,0},{12,4},{16,24},{20,28},{24,16},{28,20},{32,40},... | collective-permute-start | bytes 110600 | tf_op jit(solution)/shard_map/ppermute | solution.py:442
  10.3 0.8 %collective-permute-start.4 = (bf16[144,128]{1,0:T(8,128)(2,1)S(1)}, bf16[144,128]{1,0:T(8,128)(2,1)S(1)}, u32[]{:S(2)}, u32[]{:S(2)}) collective-permute-start(bf16[144,128]{1,0:T(8,128)(2,1)S(1)} %extend.1.refs_0_), channel_id=1, source_target_pairs={{0,12},{4,8},{8,4},{12,0},{16,28},{20,24},{24,20},{28,16},{32,44},... | collective-permute-start | bytes 110600 | tf_op jit(solution)/shard_map/ppermute | solution.py:442
  11.1 9.5 %project.1 = (f32[8,144,128]{2,1,0:T(8,128)S(1)}, bf16[8192,1024]{1,0:T(8,128)(2,1)S(1)}, bf16[144,8192]{1,0:T(8,128)(2,1)S(1)}) custom-call(bf16[128,8192]{1,0:T(8,128)(2,1)} %bitcast.9, bf16[2,8320]{1,0:T(2,128)(2,1)S(1)} %collective-permute-done.near_ref, bf16[2,8320]{1,0:T(2,128)(2,1)S(1)} %collective-permute-done.1.far_ref, bf16[65536,128]{1,0:T(8,128)(2,1)} %bitcast.7, ...), custom_call_target="tpu_custom_call" | custom-call | tf_op jit(solution)/shard_map/project/pallas_call | solution.py:188
  20.6 0.0 collective-permute-done.2.refs_1_
  20.6 0.0 collective-permute-done.3.refs_2_
  20.6 0.0 collective-permute-done.4.refs_3_
  20.6 0.2 combine.1
  20.8 16.5 %all_to_all.10.pieces_ref = bf16[8,144,128]{2,1,0:T(8,128)(2,1)S(1)} all-to-all(bf16[8,144,128]{2,1,0:T(8,128)(2,1)S(1)} %combine.1), channel_id=1, replica_groups={{0,16,32,48,64,80,96,112},{4,20,36,52,68,84,100,116},{8,24,40,56,72,88,..., dimensions={0} | all-to-all | bytes 589824 | tf_op jit(solution)/shard_map/all_to_all | solution.py:448
  37.4 11.5 %all_to_all.11.img_ref = bf16[8,144,128]{2,1,0:T(8,128)(2,1)S(1)} all-to-all(bf16[8,144,128]{2,1,0:T(8,128)(2,1)S(1)} %total.1), channel_id=1, replica_groups={{0,16,32,48,64,80,96,112},{4,20,36,52,68,84,100,116},{8,24,40,56,72,88,..., dimensions={0} | all-to-all | bytes 589824 | tf_op jit(solution)/shard_map/all_to_all | solution.py:449
  48.9 0.2 pick.1
  49.1 0.8 %collective-permute-start.5 = (bf16[128,128]{1,0:T(8,128)(2,1)S(1)}, bf16[128,128]{1,0:T(8,128)(2,1)S(1)}, u32[]{:S(2)}, u32[]{:S(2)}) collective-permute-start(bf16[128,128]{1,0:T(8,128)(2,1)S(1)} %get-tuple-element.21), channel_id=1, source_target_pairs={{0,4},{4,0},{8,12},{12,8},{16,20},{20,16},{24,28},{28,24},{32,36},... | collective-permute-start | bytes 98312 | tf_op jit(solution)/shard_map/ppermute | solution.py:452
  50.0 1.0 %collective-permute-start.6 = (bf16[128,128]{1,0:T(8,128)(2,1)S(1)}, bf16[128,128]{1,0:T(8,128)(2,1)S(1)}, u32[]{:S(2)}, u32[]{:S(2)}) collective-permute-start(bf16[128,128]{1,0:T(8,128)(2,1)S(1)} %get-tuple-element.22), channel_id=1, source_target_pairs={{0,8},{4,12},{8,0},{12,4},{16,24},{20,28},{24,16},{28,20},{32,40},... | collective-permute-start | bytes 98312 | tf_op jit(solution)/shard_map/ppermute | solution.py:452
  51.0 1.7 %collective-permute-start.7 = (bf16[128,128]{1,0:T(8,128)(2,1)S(1)}, bf16[128,128]{1,0:T(8,128)(2,1)S(1)}, u32[]{:S(2)}, u32[]{:S(2)}) collective-permute-start(bf16[128,128]{1,0:T(8,128)(2,1)S(1)} %get-tuple-element.23), channel_id=1, source_target_pairs={{0,12},{4,8},{8,4},{12,0},{16,28},{20,24},{24,20},{28,16},{32,44},... | collective-permute-start | bytes 98312 | tf_op jit(solution)/shard_map/ppermute | solution.py:452
  52.7 11.3 %fold.1.flat_ref = bf16[8192,512]{1,0:T(8,128)(2,1)S(1)} custom-call(bf16[8192,1024]{1,0:T(8,128)(2,1)S(1)} %get-tuple-element.18.flat_ref, f32[80,128]{1,0:T(8,128)S(1)} %get-tuple-element.15.table_ref), custom_call_target="tpu_custom_call" | custom-call | tf_op jit(solution)/shard_map/fold/pallas_call | solution.py:236
  64.0 5.0 %update.1 = bf16[128,8192]{1,0:T(8,128)(2,1)} custom-call(bf16[8,144,128]{2,1,0:T(8,128)(2,1)S(1)} %all_to_all.11.img_ref, f32[80,128]{1,0:T(8,128)S(1)} %get-tuple-element.15.table_ref, bf16[8192,512]{1,0:T(8,128)(2,1)S(1)} %fold.1.flat_ref, bf16[144,8192]{1,0:T(8,128)(2,1)S(1)} %get-tuple-element.19.vol_ref), custom_call_target="tpu_custom_call" | custom-call | tf_op jit(solution)/shard_map/update/pallas_call | solution.py:411
  69.0 0.0 collective-permute-done.5.refs_1_
  69.0 0.0 collective-permute-done.6.refs_2_
  69.1 0.0 collective-permute-done.7.refs_3_
  69.1 0.7 choose.1
  (2 shorter events, 0.1 us)
Async XLA Ops:
  2.5 1.4 %collective-permute-start = (bf16[2,8320]{1,0:T(2,128)(2,1)S(1)}, bf16[2,8320]{1,0:T(2,128)(2,1)S(1)}, u32[]{:S(2)}, u32[]{:S(2)}) collective-permute-start(bf16[2,8320]{1,0:T(2,128)(2,1)S(1)} %get-tuple-element.13), channel_id=1, source_target_pairs={{0,1},{1,0},{2,3},{3,2},{4,5},{5,4},{6,7},{7,6},{8,9},{9,8},{10,11... | collective-permute-start | bytes 99848 | tf_op jit(solution)/shard_map/ppermute | solution.py:437
  2.6 4.9 %collective-permute-start.1 = (bf16[2,8320]{1,0:T(2,128)(2,1)S(1)}, bf16[2,8320]{1,0:T(2,128)(2,1)S(1)}, u32[]{:S(2)}, u32[]{:S(2)}) collective-permute-start(bf16[2,8320]{1,0:T(2,128)(2,1)S(1)} %get-tuple-element.14), channel_id=1, source_target_pairs={{0,3},{1,2},{2,1},{3,0},{4,7},{5,6},{6,5},{7,4},{8,11},{9,10},{10,... | collective-permute-start | bytes 99848 | tf_op jit(solution)/shard_map/ppermute | solution.py:438
  7.6 13.1 %collective-permute-start.2 = (bf16[144,128]{1,0:T(8,128)(2,1)S(1)}, bf16[144,128]{1,0:T(8,128)(2,1)S(1)}, u32[]{:S(2)}, u32[]{:S(2)}) collective-permute-start(bf16[144,128]{1,0:T(8,128)(2,1)S(1)} %extend.1.refs_0_), channel_id=1, source_target_pairs={{0,4},{4,0},{8,12},{12,8},{16,20},{20,16},{24,28},{28,24},{32,36},... | collective-permute-start | bytes 110600 | tf_op jit(solution)/shard_map/ppermute | solution.py:442
  8.4 12.3 %collective-permute-start.3 = (bf16[144,128]{1,0:T(8,128)(2,1)S(1)}, bf16[144,128]{1,0:T(8,128)(2,1)S(1)}, u32[]{:S(2)}, u32[]{:S(2)}) collective-permute-start(bf16[144,128]{1,0:T(8,128)(2,1)S(1)} %extend.1.refs_0_), channel_id=1, source_target_pairs={{0,8},{4,12},{8,0},{12,4},{16,24},{20,28},{24,16},{28,20},{32,40},... | collective-permute-start | bytes 110600 | tf_op jit(solution)/shard_map/ppermute | solution.py:442
  10.3 10.3 %collective-permute-start.4 = (bf16[144,128]{1,0:T(8,128)(2,1)S(1)}, bf16[144,128]{1,0:T(8,128)(2,1)S(1)}, u32[]{:S(2)}, u32[]{:S(2)}) collective-permute-start(bf16[144,128]{1,0:T(8,128)(2,1)S(1)} %extend.1.refs_0_), channel_id=1, source_target_pairs={{0,12},{4,8},{8,4},{12,0},{16,28},{20,24},{24,20},{28,16},{32,44},... | collective-permute-start | bytes 110600 | tf_op jit(solution)/shard_map/ppermute | solution.py:442
  49.1 19.9 %collective-permute-start.5 = (bf16[128,128]{1,0:T(8,128)(2,1)S(1)}, bf16[128,128]{1,0:T(8,128)(2,1)S(1)}, u32[]{:S(2)}, u32[]{:S(2)}) collective-permute-start(bf16[128,128]{1,0:T(8,128)(2,1)S(1)} %get-tuple-element.21), channel_id=1, source_target_pairs={{0,4},{4,0},{8,12},{12,8},{16,20},{20,16},{24,28},{28,24},{32,36},... | collective-permute-start | bytes 98312 | tf_op jit(solution)/shard_map/ppermute | solution.py:452
  50.0 19.1 %collective-permute-start.6 = (bf16[128,128]{1,0:T(8,128)(2,1)S(1)}, bf16[128,128]{1,0:T(8,128)(2,1)S(1)}, u32[]{:S(2)}, u32[]{:S(2)}) collective-permute-start(bf16[128,128]{1,0:T(8,128)(2,1)S(1)} %get-tuple-element.22), channel_id=1, source_target_pairs={{0,8},{4,12},{8,0},{12,4},{16,24},{20,28},{24,16},{28,20},{32,40},... | collective-permute-start | bytes 98312 | tf_op jit(solution)/shard_map/ppermute | solution.py:452
  51.0 18.1 %collective-permute-start.7 = (bf16[128,128]{1,0:T(8,128)(2,1)S(1)}, bf16[128,128]{1,0:T(8,128)(2,1)S(1)}, u32[]{:S(2)}, u32[]{:S(2)}) collective-permute-start(bf16[128,128]{1,0:T(8,128)(2,1)S(1)} %get-tuple-element.23), channel_id=1, source_target_pairs={{0,12},{4,8},{8,4},{12,0},{16,28},{20,24},{24,20},{28,16},{32,44},... | collective-permute-start | bytes 98312 | tf_op jit(solution)/shard_map/ppermute | solution.py:452

commit v4 on v3

--- a/solution.py
+++ b/solution.py
@@ -208,16 +208,17 @@
 def fold_kernel(flat_ref, table_ref, out_ref):
     cells, wide = flat_ref.shape
     det = table_ref.shape[1]
+    block = 8 * PIECE
     low = lax.broadcasted_iota(jnp.int32, (1, det), 1) < det // 2
-    low_block = jnp.broadcast_to(low, (PIECE, det))
+    low_block = jnp.broadcast_to(low, (block, det))
     keeps = []
     for p in range(wide // (2 * det)):
         k = MASK + 2 * p
         line = jnp.where(low, table_ref[k : k + 1, :], table_ref[k + 1 : k + 2, :])
-        keeps.append(jnp.broadcast_to(line.astype(bf16), (PIECE, det)) > 0.5)
+        keeps.append(jnp.broadcast_to(line.astype(bf16), (block, det)) > 0.5)
 
     def step(i, carry):
-        at = pl.ds(pl.multiple_of(i * PIECE, PIECE), PIECE)
+        at = pl.ds(pl.multiple_of(i * block, block), block)
         for p, stay in enumerate(keeps):
             first = flat_ref[at, 2 * p * det : (2 * p + 1) * det]
             second = flat_ref[at, (2 * p + 1) * det : (2 * p + 2) * det]
@@ -228,7 +229,7 @@
             )
         return carry
 
-    lax.fori_loop(0, cells // PIECE, step, 0)
+    lax.fori_loop(0, cells // block, step, 0)
 
 
 def fold(flat, table):

time: 70.1 us -> 62.1 us (0.89)
  Pallas kernels: 28.1 us -> 20.2 us
    pallas_call x1, Pallas kernels: 11.3 us -> 3.39 us  [fold(): pl.pallas_call(fold_kernel, in_specs=[VMEM, VMEM], out_specs=VMEM, out_sh...]
  transfers between devices with their start and end apart: 8 -> 8, of which waited for: 1 -> 1; matrix products, arithmetic and copies ran while one was open for 0% -> 0% of each run, Pallas kernels for 37% -> 29%
where the time goes in v4:
time: 62.1 us; the launch traced here: 61.8 us
  blocking collectives  28 us (45%)
  Pallas kernels  20.2 us (33%)
  starting transfers between devices  8.56 us (14%)
  waiting for transfers between devices  3.61 us (6%)
  between operations  1.38 us (2%)
    all_to_all x1, blocking collectives, local(): lax.all_to_all(part, 'orient', 0, 0, axis_index_groups=classes, tiled=True)  16.5 us
    all_to_all x1, blocking collectives, local(): lax.all_to_all(total(pieces), 'orient', 0, 0, axis_index_groups=classes,...  11.5 us
    pallas_call x1, Pallas kernels, project(): pl.pallas_call(project_kernel, in_specs=[HBM, VMEM, VMEM, HBM, VMEM], out...  9.49 us
    pallas_call x1, Pallas kernels, update(): pl.pallas_call(update_kernel, in_specs=[VMEM] * 4, out_specs=HBM, out_sha...  5 us
    ppermute x1, waiting for transfers between devices, local(): far = lax.ppermute(far, 'slab', [(i, slabs - 1 - i) for i in range(slabs)])  3.59 us
    ppermute x3, starting transfers between devices, local(): lax.ppermute(picked[s], 'orient', swaps[s])  3.57 us
    ppermute x3, starting transfers between devices, local(): lax.ppermute(meas_ext, 'orient', swaps[s])  3.57 us
    pallas_call x1, Pallas kernels, fold(): pl.pallas_call(fold_kernel, in_specs=[VMEM, VMEM], out_specs=VMEM, out_sh...  3.39 us
  transfers between devices with their start and end apart: 8, of which 1 were waited for; matrix products, arithmetic and copies ran while one was open for 0% of the time, Pallas kernels for 29%

profile of v4, /device:TPU:24, one launch (start us, length us, event | category | flops | bytes accessed | tf_op | source)
XLA Modules:
  0.0 61.8 jit_solution(14207859618741585234)
XLA Ops:
  1.3 1.2 %prepare.1 = (bf16[2,8320]{1,0:T(2,128)(2,1)S(1)}, bf16[2,8320]{1,0:T(2,128)(2,1)S(1)}, f32[128,128]{1,0:T(8,128)S(1)}, f32[80,128]{1,0:T(8,128)S(1)}) custom-call(bf16[128,8192]{1,0:T(8,128)(2,1)} %bitcast.8, f32[128,128]{1,0:T(8,128)} %bitcast.11, s32[8]{0:T(128)} %bitcast.13, s32[8]{0:T(128)} %bitcast.14, s32[32]{0:T(128)} %refs_4_.1, f32[1]{0:T(128)S(6)} %copy.9.refs_5_), custom_call_target="tpu_custom_call" | custom-call | tf_op jit(solution)/shard_map/prepare/pallas_call | solution.py:105
  2.5 0.1 collective-permute-start
  2.6 1.3 %collective-permute-start.1 = (bf16[2,8320]{1,0:T(2,128)(2,1)S(1)}, bf16[2,8320]{1,0:T(2,128)(2,1)S(1)}, u32[]{:S(2)}, u32[]{:S(2)}) collective-permute-start(bf16[2,8320]{1,0:T(2,128)(2,1)S(1)} %get-tuple-element.14), channel_id=1, source_target_pairs={{0,3},{1,2},{2,1},{3,0},{4,7},{5,6},{6,5},{7,4},{8,11},{9,10},{10,... | collective-permute-start | bytes 99848 | tf_op jit(solution)/shard_map/ppermute | solution.py:439
  3.9 0.0 collective-permute-done.near_ref
  3.9 3.6 %collective-permute-done.1.far_ref = bf16[2,8320]{1,0:T(2,128)(2,1)S(1)} collective-permute-done((bf16[2,8320]{1,0:T(2,128)(2,1)S(1)}, bf16[2,8320]{1,0:T(2,128)(2,1)S(1)}, u32[]{:S(2)}, u32[]{:S(2)}) %collective-permute-start.1) | collective-permute-done | bytes 33312 | tf_op jit(solution)/shard_map/ppermute | solution.py:439
  7.6 0.8 %collective-permute-start.2 = (bf16[144,128]{1,0:T(8,128)(2,1)S(1)}, bf16[144,128]{1,0:T(8,128)(2,1)S(1)}, u32[]{:S(2)}, u32[]{:S(2)}) collective-permute-start(bf16[144,128]{1,0:T(8,128)(2,1)S(1)} %extend.1.refs_0_), channel_id=1, source_target_pairs={{0,4},{4,0},{8,12},{12,8},{16,20},{20,16},{24,28},{28,24},{32,36},... | collective-permute-start | bytes 110600 | tf_op jit(solution)/shard_map/ppermute | solution.py:443
  8.4 1.9 %collective-permute-start.3 = (bf16[144,128]{1,0:T(8,128)(2,1)S(1)}, bf16[144,128]{1,0:T(8,128)(2,1)S(1)}, u32[]{:S(2)}, u32[]{:S(2)}) collective-permute-start(bf16[144,128]{1,0:T(8,128)(2,1)S(1)} %extend.1.refs_0_), channel_id=1, source_target_pairs={{0,8},{4,12},{8,0},{12,4},{16,24},{20,28},{24,16},{28,20},{32,40},... | collective-permute-start | bytes 110600 | tf_op jit(solution)/shard_map/ppermute | solution.py:443
  10.3 0.8 %collective-permute-start.4 = (bf16[144,128]{1,0:T(8,128)(2,1)S(1)}, bf16[144,128]{1,0:T(8,128)(2,1)S(1)}, u32[]{:S(2)}, u32[]{:S(2)}) collective-permute-start(bf16[144,128]{1,0:T(8,128)(2,1)S(1)} %extend.1.refs_0_), channel_id=1, source_target_pairs={{0,12},{4,8},{8,4},{12,0},{16,28},{20,24},{24,20},{28,16},{32,44},... | collective-permute-start | bytes 110600 | tf_op jit(solution)/shard_map/ppermute | solution.py:443
  11.1 9.5 %project.1 = (f32[8,144,128]{2,1,0:T(8,128)S(1)}, bf16[8192,1024]{1,0:T(8,128)(2,1)S(1)}, bf16[144,8192]{1,0:T(8,128)(2,1)S(1)}) custom-call(bf16[128,8192]{1,0:T(8,128)(2,1)} %bitcast.9, bf16[2,8320]{1,0:T(2,128)(2,1)S(1)} %collective-permute-done.near_ref, bf16[2,8320]{1,0:T(2,128)(2,1)S(1)} %collective-permute-done.1.far_ref, bf16[65536,128]{1,0:T(8,128)(2,1)} %bitcast.7, ...), custom_call_target="tpu_custom_call" | custom-call | tf_op jit(solution)/shard_map/project/pallas_call | solution.py:188
  20.6 0.0 collective-permute-done.2.refs_1_
  20.6 0.0 collective-permute-done.3.refs_2_
  20.6 0.0 collective-permute-done.4.refs_3_
  20.6 0.2 combine.1
  20.8 16.5 %all_to_all.10.pieces_ref = bf16[8,144,128]{2,1,0:T(8,128)(2,1)S(1)} all-to-all(bf16[8,144,128]{2,1,0:T(8,128)(2,1)S(1)} %combine.1), channel_id=1, replica_groups={{0,16,32,48,64,80,96,112},{4,20,36,52,68,84,100,116},{8,24,40,56,72,88,..., dimensions={0} | all-to-all | bytes 589824 | tf_op jit(solution)/shard_map/all_to_all | solution.py:449
  37.4 11.5 %all_to_all.11.img_ref = bf16[8,144,128]{2,1,0:T(8,128)(2,1)S(1)} all-to-all(bf16[8,144,128]{2,1,0:T(8,128)(2,1)S(1)} %total.1), channel_id=1, replica_groups={{0,16,32,48,64,80,96,112},{4,20,36,52,68,84,100,116},{8,24,40,56,72,88,..., dimensions={0} | all-to-all | bytes 589824 | tf_op jit(solution)/shard_map/all_to_all | solution.py:450
  48.9 0.2 pick.1
  49.1 0.8 %collective-permute-start.5 = (bf16[128,128]{1,0:T(8,128)(2,1)S(1)}, bf16[128,128]{1,0:T(8,128)(2,1)S(1)}, u32[]{:S(2)}, u32[]{:S(2)}) collective-permute-start(bf16[128,128]{1,0:T(8,128)(2,1)S(1)} %get-tuple-element.21), channel_id=1, source_target_pairs={{0,4},{4,0},{8,12},{12,8},{16,20},{20,16},{24,28},{28,24},{32,36},... | collective-permute-start | bytes 98312 | tf_op jit(solution)/shard_map/ppermute | solution.py:453
  50.0 1.0 %collective-permute-start.6 = (bf16[128,128]{1,0:T(8,128)(2,1)S(1)}, bf16[128,128]{1,0:T(8,128)(2,1)S(1)}, u32[]{:S(2)}, u32[]{:S(2)}) collective-permute-start(bf16[128,128]{1,0:T(8,128)(2,1)S(1)} %get-tuple-element.22), channel_id=1, source_target_pairs={{0,8},{4,12},{8,0},{12,4},{16,24},{20,28},{24,16},{28,20},{32,40},... | collective-permute-start | bytes 98312 | tf_op jit(solution)/shard_map/ppermute | solution.py:453
  51.0 1.7 %collective-permute-start.7 = (bf16[128,128]{1,0:T(8,128)(2,1)S(1)}, bf16[128,128]{1,0:T(8,128)(2,1)S(1)}, u32[]{:S(2)}, u32[]{:S(2)}) collective-permute-start(bf16[128,128]{1,0:T(8,128)(2,1)S(1)} %get-tuple-element.23), channel_id=1, source_target_pairs={{0,12},{4,8},{8,4},{12,0},{16,28},{20,24},{24,20},{28,16},{32,44},... | collective-permute-start | bytes 98312 | tf_op jit(solution)/shard_map/ppermute | solution.py:453
  52.7 3.4 %fold.1.flat_ref = bf16[8192,512]{1,0:T(8,128)(2,1)S(1)} custom-call(bf16[8192,1024]{1,0:T(8,128)(2,1)S(1)} %get-tuple-element.18.flat_ref, f32[80,128]{1,0:T(8,128)S(1)} %get-tuple-element.15.table_ref), custom_call_target="tpu_custom_call" | custom-call | tf_op jit(solution)/shard_map/fold/pallas_call | solution.py:237
  56.1 5.0 %update.1 = bf16[128,8192]{1,0:T(8,128)(2,1)} custom-call(bf16[8,144,128]{2,1,0:T(8,128)(2,1)S(1)} %all_to_all.11.img_ref, f32[80,128]{1,0:T(8,128)S(1)} %get-tuple-element.15.table_ref, bf16[8192,512]{1,0:T(8,128)(2,1)S(1)} %fold.1.flat_ref, bf16[144,8192]{1,0:T(8,128)(2,1)S(1)} %get-tuple-element.19.vol_ref), custom_call_target="tpu_custom_call" | custom-call | tf_op jit(solution)/shard_map/update/pallas_call | solution.py:412
  61.1 0.0 collective-permute-done.5.refs_1_
  61.1 0.0 collective-permute-done.6.refs_2_
  61.1 0.0 collective-permute-done.7.refs_3_
  61.1 0.7 %choose.1 = f32[128,128]{1,0:T(8,128)} custom-call(f32[80,128]{1,0:T(8,128)S(1)} %get-tuple-element.15.table_ref, bf16[128,128]{1,0:T(8,128)(2,1)S(1)} %get-tuple-element.20.refs_0_, bf16[128,128]{1,0:T(8,128)(2,1)S(1)} %collective-permute-done.5.refs_1_, bf16[128,128]{1,0:T(8,128)(2,1)S(1)} %collective-permute-done.6.refs_2_, ...), custom_call_target="tpu_custom_call" | custom-call | tf_op jit(solution)/shard_map/choose/pallas_call | solution.py:320
  (2 shorter events, 0.1 us)
Async XLA Ops:
  2.5 1.4 %collective-permute-start = (bf16[2,8320]{1,0:T(2,128)(2,1)S(1)}, bf16[2,8320]{1,0:T(2,128)(2,1)S(1)}, u32[]{:S(2)}, u32[]{:S(2)}) collective-permute-start(bf16[2,8320]{1,0:T(2,128)(2,1)S(1)} %get-tuple-element.13), channel_id=1, source_target_pairs={{0,1},{1,0},{2,3},{3,2},{4,5},{5,4},{6,7},{7,6},{8,9},{9,8},{10,11... | collective-permute-start | bytes 99848 | tf_op jit(solution)/shard_map/ppermute | solution.py:438
  2.6 4.9 %collective-permute-start.1 = (bf16[2,8320]{1,0:T(2,128)(2,1)S(1)}, bf16[2,8320]{1,0:T(2,128)(2,1)S(1)}, u32[]{:S(2)}, u32[]{:S(2)}) collective-permute-start(bf16[2,8320]{1,0:T(2,128)(2,1)S(1)} %get-tuple-element.14), channel_id=1, source_target_pairs={{0,3},{1,2},{2,1},{3,0},{4,7},{5,6},{6,5},{7,4},{8,11},{9,10},{10,... | collective-permute-start | bytes 99848 | tf_op jit(solution)/shard_map/ppermute | solution.py:439
  7.6 13.1 %collective-permute-start.2 = (bf16[144,128]{1,0:T(8,128)(2,1)S(1)}, bf16[144,128]{1,0:T(8,128)(2,1)S(1)}, u32[]{:S(2)}, u32[]{:S(2)}) collective-permute-start(bf16[144,128]{1,0:T(8,128)(2,1)S(1)} %extend.1.refs_0_), channel_id=1, source_target_pairs={{0,4},{4,0},{8,12},{12,8},{16,20},{20,16},{24,28},{28,24},{32,36},... | collective-permute-start | bytes 110600 | tf_op jit(solution)/shard_map/ppermute | solution.py:443
  8.4 12.3 %collective-permute-start.3 = (bf16[144,128]{1,0:T(8,128)(2,1)S(1)}, bf16[144,128]{1,0:T(8,128)(2,1)S(1)}, u32[]{:S(2)}, u32[]{:S(2)}) collective-permute-start(bf16[144,128]{1,0:T(8,128)(2,1)S(1)} %extend.1.refs_0_), channel_id=1, source_target_pairs={{0,8},{4,12},{8,0},{12,4},{16,24},{20,28},{24,16},{28,20},{32,40},... | collective-permute-start | bytes 110600 | tf_op jit(solution)/shard_map/ppermute | solution.py:443
  10.3 10.3 %collective-permute-start.4 = (bf16[144,128]{1,0:T(8,128)(2,1)S(1)}, bf16[144,128]{1,0:T(8,128)(2,1)S(1)}, u32[]{:S(2)}, u32[]{:S(2)}) collective-permute-start(bf16[144,128]{1,0:T(8,128)(2,1)S(1)} %extend.1.refs_0_), channel_id=1, source_target_pairs={{0,12},{4,8},{8,4},{12,0},{16,28},{20,24},{24,20},{28,16},{32,44},... | collective-permute-start | bytes 110600 | tf_op jit(solution)/shard_map/ppermute | solution.py:443
  49.1 12.0 %collective-permute-start.5 = (bf16[128,128]{1,0:T(8,128)(2,1)S(1)}, bf16[128,128]{1,0:T(8,128)(2,1)S(1)}, u32[]{:S(2)}, u32[]{:S(2)}) collective-permute-start(bf16[128,128]{1,0:T(8,128)(2,1)S(1)} %get-tuple-element.21), channel_id=1, source_target_pairs={{0,4},{4,0},{8,12},{12,8},{16,20},{20,16},{24,28},{28,24},{32,36},... | collective-permute-start | bytes 98312 | tf_op jit(solution)/shard_map/ppermute | solution.py:453
  50.0 11.2 %collective-permute-start.6 = (bf16[128,128]{1,0:T(8,128)(2,1)S(1)}, bf16[128,128]{1,0:T(8,128)(2,1)S(1)}, u32[]{:S(2)}, u32[]{:S(2)}) collective-permute-start(bf16[128,128]{1,0:T(8,128)(2,1)S(1)} %get-tuple-element.22), channel_id=1, source_target_pairs={{0,8},{4,12},{8,0},{12,4},{16,24},{20,28},{24,16},{28,20},{32,40},... | collective-permute-start | bytes 98312 | tf_op jit(solution)/shard_map/ppermute | solution.py:453
  51.0 10.2 %collective-permute-start.7 = (bf16[128,128]{1,0:T(8,128)(2,1)S(1)}, bf16[128,128]{1,0:T(8,128)(2,1)S(1)}, u32[]{:S(2)}, u32[]{:S(2)}) collective-permute-start(bf16[128,128]{1,0:T(8,128)(2,1)S(1)} %get-tuple-element.23), channel_id=1, source_target_pairs={{0,12},{4,8},{8,4},{12,0},{16,28},{20,24},{24,20},{28,16},{32,44},... | collective-permute-start | bytes 98312 | tf_op jit(solution)/shard_map/ppermute | solution.py:453

commit v5 on v3

--- a/solution.py
+++ b/solution.py
@@ -18,7 +18,7 @@
 f32 = jnp.float32
 
 
-PIECE = 64
+CHUNKS = 8
 SMALL = 4 << 20
 
 MASK = 0
@@ -118,6 +118,7 @@
             pltpu.SemaphoreType.DMA((6,)),
         ],
         compiler_params=pltpu.CompilerParams(vmem_limit_bytes=SMALL),
+        cost_estimate=pl.CostEstimate(flops=40 << 30, transcendentals=0, bytes_accessed=1 << 20),
         name="prepare",
     )(*(keep(x) for x in (vol, meas, start, length, slot_image)), relax)
 
@@ -149,98 +150,42 @@
     )(meas, near, far)
 
 
-def project_kernel(vol_hbm, near_ref, far_ref, rays_hbm, table_ref, proj_ref, flat_ref, vol_ref, buf, acc, vsem, rsem):
-    chunks = rsem.shape[0]
+def project_kernel(vol_hbm, near_ref, far_ref, rays_ref, table_ref, proj_ref, flat_ref, vol_ref, acc, sem):
     rows, cells = vol_hbm.shape
-    chunk = cells // chunks
-    refl = buf.shape[0] // cells
-    det = buf.shape[1]
-
-    def copies(i):
-        at = slice(i * chunk, (i + 1) * chunk)
-        wide = slice(i * chunk * refl, (i + 1) * chunk * refl)
-        return (
-            pltpu.make_async_copy(vol_hbm.at[:, at], vol_ref.at[0:rows, at], vsem.at[i]),
-            pltpu.make_async_copy(rays_hbm.at[wide], buf.at[wide], rsem.at[i]),
-        )
-
-    for i in range(chunks):
-        for copy in copies(i):
-            copy.start()
+    refl, det = rays_ref.shape[1:]
+    chunk = cells // CHUNKS
+    copy = pltpu.make_async_copy(vol_hbm, vol_ref.at[0:rows], sem)
+    copy.start()
     even = jnp.bitwise_and(lax.axis_index("slab"), 1) == 0
     vol_ref[rows:, :] = halo_rows(near_ref[:, 0:cells], far_ref[:, 0:cells], even)
-    for i in range(chunks):
-        for copy in copies(i):
+    for i in range(CHUNKS):
+        at = slice(i * chunk, (i + 1) * chunk)
+        flat_ref[at, :] = rays_ref[at].reshape(chunk, refl * det)
+        if i == 0:
             copy.wait()
-        at = slice(i * chunk, (i + 1) * chunk)
-        for j in range(i * chunk, (i + 1) * chunk, PIECE):
-            flat_ref[j : j + PIECE, :] = buf[j * refl : (j + PIECE) * refl].reshape(PIECE, refl * det)
         part = jnp.dot(vol_ref[:, at], flat_ref[at, :], preferred_element_type=f32)
         acc[...] = part if i == 0 else acc[...] + part
     for k in range(refl):
         proj_ref[k] = acc[:, k * det : (k + 1) * det] * table_ref[MASK + k : MASK + k + 1, :]
 
 
-def project(vol, near, far, rays, table, chunk=1024):
+def project(vol, near, far, rays, table):
     rows, cells = vol.shape
     refl, det = rays.shape[1:]
     ext = rows + HALO
     return pl.pallas_call(
         project_kernel,
-        in_specs=[HBM, VMEM, VMEM, HBM, VMEM],
+        in_specs=[HBM, VMEM, VMEM, VMEM, VMEM],
         out_specs=(VMEM, VMEM, VMEM),
         out_shape=(
             jax.ShapeDtypeStruct((refl, ext, det), f32),
             pltpu.VMEM((cells, refl * det), bf16),
             pltpu.VMEM((ext, cells), bf16),
         ),
-        scratch_shapes=[
-            pltpu.VMEM((cells * refl, det), bf16),
-            pltpu.VMEM((ext, refl * det), f32),
-            pltpu.SemaphoreType.DMA((cells // chunk,)),
-            pltpu.SemaphoreType.DMA((cells // chunk,)),
-        ],
-        compiler_params=pltpu.CompilerParams(vmem_limit_bytes=24 << 20),
+        scratch_shapes=[pltpu.VMEM((ext, refl * det), f32), pltpu.SemaphoreType.DMA],
+        compiler_params=pltpu.CompilerParams(vmem_limit_bytes=8 << 20),
         name="project",
-    )(keep(vol), near, far, keep(rays.reshape(cells * refl, det)), table)
-
-
-def fold_kernel(flat_ref, table_ref, out_ref):
-    cells, wide = flat_ref.shape
-    det = table_ref.shape[1]
-    low = lax.broadcasted_iota(jnp.int32, (1, det), 1) < det // 2
-    low_block = jnp.broadcast_to(low, (PIECE, det))
-    keeps = []
-    for p in range(wide // (2 * det)):
-        k = MASK + 2 * p
-        line = jnp.where(low, table_ref[k : k + 1, :], table_ref[k + 1 : k + 2, :])
-        keeps.append(jnp.broadcast_to(line.astype(bf16), (PIECE, det)) > 0.5)
-
-    def step(i, carry):
-        at = pl.ds(pl.multiple_of(i * PIECE, PIECE), PIECE)
-        for p, stay in enumerate(keeps):
-            first = flat_ref[at, 2 * p * det : (2 * p + 1) * det]
-            second = flat_ref[at, (2 * p + 1) * det : (2 * p + 2) * det]
-            straight = jnp.where(low_block, first, second)
-            crossed = jnp.where(low_block, second, first)
-            out_ref[at, p * det : (p + 1) * det] = jnp.where(
-                stay, straight, pltpu.roll(crossed, det // 2, 1)
-            )
-        return carry
-
-    lax.fori_loop(0, cells // PIECE, step, 0)
-
-
-def fold(flat, table):
-    cells, wide = flat.shape
-    return pl.pallas_call(
-        fold_kernel,
-        in_specs=[VMEM, VMEM],
-        out_specs=VMEM,
-        out_shape=pltpu.VMEM((cells, wide // 2), bf16),
-        compiler_params=pltpu.CompilerParams(vmem_limit_bytes=SMALL),
-        name="fold",
-    )(flat, table)
+    )(keep(vol), near, far, rays, table)
 
 
 def combine_kernel(proj_ref, table_ref, *refs):
@@ -336,15 +281,9 @@
     steps = cells // chunk
     sends = osem.shape[0]
 
-    low = lax.broadcasted_iota(jnp.int32, (1, det), 1) < det // 2
-    parts = []
-    for k in range(0, refl, 2):
-        first = img_ref[k].astype(f32) * table_ref[MASK + k : MASK + k + 1, :]
-        second = img_ref[k + 1].astype(f32) * table_ref[MASK + k + 1 : MASK + k + 2, :]
-        straight = jnp.where(low, first, second)
-        crossed = jnp.where(low, second, first)
-        parts.append((straight + pltpu.roll(crossed, det // 2, 1)).astype(bf16))
-    img = jnp.concatenate(parts, axis=1)
+    img = jnp.concatenate(
+        [img_ref[k] * table_ref[MASK + k : MASK + k + 1, :].astype(bf16) for k in range(refl)], axis=1
+    )
     scale = table_ref[SCALE : SCALE + 1, 0:1]
 
     place = lax.broadcasted_iota(jnp.int32, (ext, det), 0)
@@ -442,7 +381,6 @@
     gathered = [meas_ext] + [lax.ppermute(meas_ext, "orient", swaps[s]) for s in range(1, FRAMES)]
 
     proj, flat, vol_ext = project(vol, near, far, rays, table)
-    flat = fold(flat, table)
 
     part = combine(proj, table, gathered)
     pieces = lax.all_to_all(part, "orient", 0, 0, axis_index_groups=classes, tiled=True)

time: 70.1 us -> 60.9 us (0.87)
  Pallas kernels: 28.1 us -> 18.9 us
    pallas_call x2 -> x1, Pallas kernels: 20.8 us -> 7.66 us  [project(): pl.pallas_call(project_kernel, in_specs=[HBM, VMEM, VMEM, VMEM, VMEM], ou...]
    pallas_call x1, Pallas kernels: 5 us -> 8.78 us  [update(): pl.pallas_call(update_kernel, in_specs=[VMEM] * 4, out_specs=HBM, out_sha...]
  transfers between devices with their start and end apart: 8 -> 8, of which waited for: 1 -> 1; matrix products, arithmetic and copies ran while one was open for 0% -> 0% of each run, Pallas kernels for 37% -> 27%
where the time goes in v5:
time: 60.9 us; the launch traced here: 60.6 us
  blocking collectives  28 us (46%)
  Pallas kernels  18.9 us (31%)
  starting transfers between devices  8.56 us (14%)
  waiting for transfers between devices  3.61 us (6%)
  between operations  1.42 us (2%)
    all_to_all x1, blocking collectives, local(): lax.all_to_all(part, 'orient', 0, 0, axis_index_groups=classes, tiled=True)  16.5 us
    all_to_all x1, blocking collectives, local(): lax.all_to_all(total(pieces), 'orient', 0, 0, axis_index_groups=classes,...  11.5 us
    pallas_call x1, Pallas kernels, update(): pl.pallas_call(update_kernel, in_specs=[VMEM] * 4, out_specs=HBM, out_sha...  8.78 us
    pallas_call x1, Pallas kernels, project(): pl.pallas_call(project_kernel, in_specs=[HBM, VMEM, VMEM, VMEM, VMEM], ou...  7.66 us
    ppermute x1, waiting for transfers between devices, local(): far = lax.ppermute(far, 'slab', [(i, slabs - 1 - i) for i in range(slabs)])  3.59 us
    ppermute x3, starting transfers between devices, local(): lax.ppermute(picked[s], 'orient', swaps[s])  3.57 us
    ppermute x3, starting transfers between devices, local(): lax.ppermute(meas_ext, 'orient', swaps[s])  3.57 us
    pallas_call x1, Pallas kernels, prepare(): pl.pallas_call(lambda *refs: prepare_kernel(step_gain, slabs, *refs), in_...  1.37 us
  transfers between devices with their start and end apart: 8, of which 1 were waited for; matrix products, arithmetic and copies ran while one was open for 0% of the time, Pallas kernels for 27%

profile of v5, /device:TPU:24, one launch (start us, length us, event | category | flops | bytes accessed | tf_op | source)
XLA Modules:
  0.0 60.6 jit_solution(7325091173080715294)
XLA Ops:
  1.3 0.0 slice-start
  1.3 0.0 slice-start.1
  1.3 0.0 slice-start.2
  1.3 0.0 slice-start.3
  1.3 1.4 %prepare.1 = (bf16[2,8320]{1,0:T(2,128)(2,1)S(1)}, bf16[2,8320]{1,0:T(2,128)(2,1)S(1)}, f32[128,128]{1,0:T(8,128)S(1)}, f32[80,128]{1,0:T(8,128)S(1)}) custom-call(bf16[128,8192]{1,0:T(8,128)(2,1)} %bitcast.8, f32[128,128]{1,0:T(8,128)} %bitcast.12, s32[8]{0:T(128)} %bitcast.13, s32[8]{0:T(128)} %bitcast.14, s32[32]{0:T(128)} %refs_4_.1, f32[1]{0:T(128)S(6)} %copy.9.refs_5_), custom_call_target="tpu_custom_call" | custom-call | flops 42949672960 | bytes 1048576 | tf_op jit(solution)/shard_map/prepare/pallas_call | solution.py:105
  2.7 0.1 collective-permute-start
  2.8 1.3 %collective-permute-start.1 = (bf16[2,8320]{1,0:T(2,128)(2,1)S(1)}, bf16[2,8320]{1,0:T(2,128)(2,1)S(1)}, u32[]{:S(2)}, u32[]{:S(2)}) collective-permute-start(bf16[2,8320]{1,0:T(2,128)(2,1)S(1)} %get-tuple-element.14), channel_id=1, source_target_pairs={{0,3},{1,2},{2,1},{3,0},{4,7},{5,6},{6,5},{7,4},{8,11},{9,10},{10,... | collective-permute-start | bytes 99848 | tf_op jit(solution)/shard_map/ppermute | solution.py:377
  4.1 0.0 collective-permute-done.near_ref
  4.1 3.6 %collective-permute-done.1.far_ref = bf16[2,8320]{1,0:T(2,128)(2,1)S(1)} collective-permute-done((bf16[2,8320]{1,0:T(2,128)(2,1)S(1)}, bf16[2,8320]{1,0:T(2,128)(2,1)S(1)}, u32[]{:S(2)}, u32[]{:S(2)}) %collective-permute-start.1) | collective-permute-done | bytes 33312 | tf_op jit(solution)/shard_map/ppermute | solution.py:377
  7.7 2.2 %collective-permute-start.4 = (bf16[144,128]{1,0:T(8,128)(2,1)S(1)}, bf16[144,128]{1,0:T(8,128)(2,1)S(1)}, u32[]{:S(2)}, u32[]{:S(2)}) collective-permute-start(bf16[144,128]{1,0:T(8,128)(2,1)S(1)} %extend.1.refs_0_), channel_id=1, source_target_pairs={{0,12},{4,8},{8,4},{12,0},{16,28},{20,24},{24,20},{28,16},{32,44},... | collective-permute-start | bytes 110600 | tf_op jit(solution)/shard_map/ppermute | solution.py:381
  9.9 0.1 collective-permute-start.3
  10.0 1.3 %collective-permute-start.2 = (bf16[144,128]{1,0:T(8,128)(2,1)S(1)}, bf16[144,128]{1,0:T(8,128)(2,1)S(1)}, u32[]{:S(2)}, u32[]{:S(2)}) collective-permute-start(bf16[144,128]{1,0:T(8,128)(2,1)S(1)} %extend.1.refs_0_), channel_id=1, source_target_pairs={{0,4},{4,0},{8,12},{12,8},{16,20},{20,16},{24,28},{28,24},{32,36},... | collective-permute-start | bytes 110600 | tf_op jit(solution)/shard_map/ppermute | solution.py:381
  11.3 0.0 slice-done
  11.3 0.0 slice-done.1
  11.3 0.0 slice-done.2
  11.3 0.0 slice-done.3
  11.3 7.7 %project.1 = (f32[8,144,128]{2,1,0:T(8,128)S(1)}, bf16[8192,1024]{1,0:T(8,128)(2,1)S(1)}, bf16[144,8192]{1,0:T(8,128)(2,1)S(1)}) custom-call(bf16[128,8192]{1,0:T(8,128)(2,1)} %bitcast.9, bf16[2,8320]{1,0:T(2,128)(2,1)S(1)} %collective-permute-done.near_ref, bf16[2,8320]{1,0:T(2,128)(2,1)S(1)} %collective-permute-done.1.far_ref, ...), custom_call_target="tpu_custom_call" | custom-call | tf_op jit(solution)/shard_map/project/pallas_call | solution.py:176
  19.0 0.0 collective-permute-done.4.refs_3_
  19.0 0.0 collective-permute-done.3.refs_2_
  19.0 0.0 collective-permute-done.2.refs_1_
  19.0 0.2 combine.1
  19.2 16.5 %all_to_all.10.pieces_ref = bf16[8,144,128]{2,1,0:T(8,128)(2,1)S(1)} all-to-all(bf16[8,144,128]{2,1,0:T(8,128)(2,1)S(1)} %combine.1), channel_id=1, replica_groups={{0,16,32,48,64,80,96,112},{4,20,36,52,68,84,100,116},{8,24,40,56,72,88,..., dimensions={0} | all-to-all | bytes 589824 | tf_op jit(solution)/shard_map/all_to_all | solution.py:386
  35.8 11.5 %all_to_all.11.img_ref = bf16[8,144,128]{2,1,0:T(8,128)(2,1)S(1)} all-to-all(bf16[8,144,128]{2,1,0:T(8,128)(2,1)S(1)} %total.1), channel_id=1, replica_groups={{0,16,32,48,64,80,96,112},{4,20,36,52,68,84,100,116},{8,24,40,56,72,88,..., dimensions={0} | all-to-all | bytes 589824 | tf_op jit(solution)/shard_map/all_to_all | solution.py:387
  47.3 0.2 pick.1
  47.5 0.8 %collective-permute-start.5 = (bf16[128,128]{1,0:T(8,128)(2,1)S(1)}, bf16[128,128]{1,0:T(8,128)(2,1)S(1)}, u32[]{:S(2)}, u32[]{:S(2)}) collective-permute-start(bf16[128,128]{1,0:T(8,128)(2,1)S(1)} %get-tuple-element.21), channel_id=1, source_target_pairs={{0,4},{4,0},{8,12},{12,8},{16,20},{20,16},{24,28},{28,24},{32,36},... | collective-permute-start | bytes 98312 | tf_op jit(solution)/shard_map/ppermute | solution.py:390
  48.3 1.0 %collective-permute-start.6 = (bf16[128,128]{1,0:T(8,128)(2,1)S(1)}, bf16[128,128]{1,0:T(8,128)(2,1)S(1)}, u32[]{:S(2)}, u32[]{:S(2)}) collective-permute-start(bf16[128,128]{1,0:T(8,128)(2,1)S(1)} %get-tuple-element.22), channel_id=1, source_target_pairs={{0,8},{4,12},{8,0},{12,4},{16,24},{20,28},{24,16},{28,20},{32,40},... | collective-permute-start | bytes 98312 | tf_op jit(solution)/shard_map/ppermute | solution.py:390
  49.3 1.7 %collective-permute-start.7 = (bf16[128,128]{1,0:T(8,128)(2,1)S(1)}, bf16[128,128]{1,0:T(8,128)(2,1)S(1)}, u32[]{:S(2)}, u32[]{:S(2)}) collective-permute-start(bf16[128,128]{1,0:T(8,128)(2,1)S(1)} %get-tuple-element.23), channel_id=1, source_target_pairs={{0,12},{4,8},{8,4},{12,0},{16,28},{20,24},{24,20},{28,16},{32,44},... | collective-permute-start | bytes 98312 | tf_op jit(solution)/shard_map/ppermute | solution.py:390
  51.1 8.8 %update.1 = bf16[128,8192]{1,0:T(8,128)(2,1)} custom-call(bf16[8,144,128]{2,1,0:T(8,128)(2,1)S(1)} %all_to_all.11.img_ref, f32[80,128]{1,0:T(8,128)S(1)} %get-tuple-element.15.table_ref, bf16[8192,1024]{1,0:T(8,128)(2,1)S(1)} %get-tuple-element.18.flat_ref, bf16[144,8192]{1,0:T(8,128)(2,1)S(1)} %get-tuple-element.19.vol_ref), custom_call_target="tpu_custom_call" | custom-call | tf_op jit(solution)/shard_map/update/pallas_call | solution.py:350
  59.9 0.0 collective-permute-done.5.refs_1_
  59.9 0.0 collective-permute-done.6.refs_2_
  59.9 0.0 collective-permute-done.7.refs_3_
  59.9 0.7 %choose.1 = f32[128,128]{1,0:T(8,128)} custom-call(f32[80,128]{1,0:T(8,128)S(1)} %get-tuple-element.15.table_ref, bf16[128,128]{1,0:T(8,128)(2,1)S(1)} %get-tuple-element.20.refs_0_, bf16[128,128]{1,0:T(8,128)(2,1)S(1)} %collective-permute-done.5.refs_1_, bf16[128,128]{1,0:T(8,128)(2,1)S(1)} %collective-permute-done.6.refs_2_, ...), custom_call_target="tpu_custom_call" | custom-call | tf_op jit(solution)/shard_map/choose/pallas_call | solution.py:264
  (3 shorter events, 0.1 us)
Async XLA Ops:
  1.3 10.0 %slice-start = ((s8[16777216]{0:T(1024)(128)(4,1)}), s8[4194304]{0:T(1024)(128)(4,1)S(1)}, s32[]{:S(2)}) async-start(s8[16777216]{0:T(1024)(128)(4,1)} %bitcast.6), calls=%async_computation.2 | async-start | bytes 8388608
  1.3 10.0 %slice-start.1 = ((s8[16777216]{0:T(1024)(128)(4,1)}), s8[4194304]{0:T(1024)(128)(4,1)S(1)}, s32[]{:S(2)}) async-start(s8[16777216]{0:T(1024)(128)(4,1)} %bitcast.6), calls=%async_computation.3 | async-start | bytes 8388608
  1.3 10.0 %slice-start.2 = ((s8[16777216]{0:T(1024)(128)(4,1)}), s8[4194304]{0:T(1024)(128)(4,1)S(1)}, s32[]{:S(2)}) async-start(s8[16777216]{0:T(1024)(128)(4,1)} %bitcast.6), calls=%async_computation.4 | async-start | bytes 8388608
  1.3 10.0 %slice-start.3 = ((s8[16777216]{0:T(1024)(128)(4,1)}), s8[4194304]{0:T(1024)(128)(4,1)S(1)}, s32[]{:S(2)}) async-start(s8[16777216]{0:T(1024)(128)(4,1)} %bitcast.6), calls=%async_computation.5 | async-start | bytes 8388608
  2.7 1.4 %collective-permute-start = (bf16[2,8320]{1,0:T(2,128)(2,1)S(1)}, bf16[2,8320]{1,0:T(2,128)(2,1)S(1)}, u32[]{:S(2)}, u32[]{:S(2)}) collective-permute-start(bf16[2,8320]{1,0:T(2,128)(2,1)S(1)} %get-tuple-element.13), channel_id=1, source_target_pairs={{0,1},{1,0},{2,3},{3,2},{4,5},{5,4},{6,7},{7,6},{8,9},{9,8},{10,11... | collective-permute-start | bytes 99848 | tf_op jit(solution)/shard_map/ppermute | solution.py:376
  2.8 4.9 %collective-permute-start.1 = (bf16[2,8320]{1,0:T(2,128)(2,1)S(1)}, bf16[2,8320]{1,0:T(2,128)(2,1)S(1)}, u32[]{:S(2)}, u32[]{:S(2)}) collective-permute-start(bf16[2,8320]{1,0:T(2,128)(2,1)S(1)} %get-tuple-element.14), channel_id=1, source_target_pairs={{0,3},{1,2},{2,1},{3,0},{4,7},{5,6},{6,5},{7,4},{8,11},{9,10},{10,... | collective-permute-start | bytes 99848 | tf_op jit(solution)/shard_map/ppermute | solution.py:377
  7.7 11.3 %collective-permute-start.4 = (bf16[144,128]{1,0:T(8,128)(2,1)S(1)}, bf16[144,128]{1,0:T(8,128)(2,1)S(1)}, u32[]{:S(2)}, u32[]{:S(2)}) collective-permute-start(bf16[144,128]{1,0:T(8,128)(2,1)S(1)} %extend.1.refs_0_), channel_id=1, source_target_pairs={{0,12},{4,8},{8,4},{12,0},{16,28},{20,24},{24,20},{28,16},{32,44},... | collective-permute-start | bytes 110600 | tf_op jit(solution)/shard_map/ppermute | solution.py:381
  9.9 9.1 %collective-permute-start.3 = (bf16[144,128]{1,0:T(8,128)(2,1)S(1)}, bf16[144,128]{1,0:T(8,128)(2,1)S(1)}, u32[]{:S(2)}, u32[]{:S(2)}) collective-permute-start(bf16[144,128]{1,0:T(8,128)(2,1)S(1)} %extend.1.refs_0_), channel_id=1, source_target_pairs={{0,8},{4,12},{8,0},{12,4},{16,24},{20,28},{24,16},{28,20},{32,40},... | collective-permute-start | bytes 110600 | tf_op jit(solution)/shard_map/ppermute | solution.py:381
  10.0 9.0 %collective-permute-start.2 = (bf16[144,128]{1,0:T(8,128)(2,1)S(1)}, bf16[144,128]{1,0:T(8,128)(2,1)S(1)}, u32[]{:S(2)}, u32[]{:S(2)}) collective-permute-start(bf16[144,128]{1,0:T(8,128)(2,1)S(1)} %extend.1.refs_0_), channel_id=1, source_target_pairs={{0,4},{4,0},{8,12},{12,8},{16,20},{20,16},{24,28},{28,24},{32,36},... | collective-permute-start | bytes 110600 | tf_op jit(solution)/shard_map/ppermute | solution.py:381
  47.5 12.4 %collective-permute-start.5 = (bf16[128,128]{1,0:T(8,128)(2,1)S(1)}, bf16[128,128]{1,0:T(8,128)(2,1)S(1)}, u32[]{:S(2)}, u32[]{:S(2)}) collective-permute-start(bf16[128,128]{1,0:T(8,128)(2,1)S(1)} %get-tuple-element.21), channel_id=1, source_target_pairs={{0,4},{4,0},{8,12},{12,8},{16,20},{20,16},{24,28},{28,24},{32,36},... | collective-permute-start | bytes 98312 | tf_op jit(solution)/shard_map/ppermute | solution.py:390
  48.3 11.6 %collective-permute-start.6 = (bf16[128,128]{1,0:T(8,128)(2,1)S(1)}, bf16[128,128]{1,0:T(8,128)(2,1)S(1)}, u32[]{:S(2)}, u32[]{:S(2)}) collective-permute-start(bf16[128,128]{1,0:T(8,128)(2,1)S(1)} %get-tuple-element.22), channel_id=1, source_target_pairs={{0,8},{4,12},{8,0},{12,4},{16,24},{20,28},{24,16},{28,20},{32,40},... | collective-permute-start | bytes 98312 | tf_op jit(solution)/shard_map/ppermute | solution.py:390
  49.3 10.6 %collective-permute-start.7 = (bf16[128,128]{1,0:T(8,128)(2,1)S(1)}, bf16[128,128]{1,0:T(8,128)(2,1)S(1)}, u32[]{:S(2)}, u32[]{:S(2)}) collective-permute-start(bf16[128,128]{1,0:T(8,128)(2,1)S(1)} %get-tuple-element.23), channel_id=1, source_target_pairs={{0,12},{4,8},{8,4},{12,0},{16,28},{20,24},{24,20},{28,16},{32,44},... | collective-permute-start | bytes 98312 | tf_op jit(solution)/shard_map/ppermute | solution.py:390

commit v6 on v5

--- a/solution.py
+++ b/solution.py
@@ -19,6 +19,7 @@
 
 
 CHUNKS = 8
+PIECE = 16
 SMALL = 4 << 20
 
 MASK = 0
@@ -158,15 +159,33 @@
     copy.start()
     even = jnp.bitwise_and(lax.axis_index("slab"), 1) == 0
     vol_ref[rows:, :] = halo_rows(near_ref[:, 0:cells], far_ref[:, 0:cells], even)
+    low = lax.broadcasted_iota(jnp.int32, (1, det), 1) < det // 2
+    low_block = jnp.broadcast_to(low, (PIECE, det))
+    stay = []
+    for k in range(MASK, MASK + refl, 2):
+        line = jnp.where(low, table_ref[k : k + 1, :], table_ref[k + 1 : k + 2, :])
+        stay.append(jnp.broadcast_to(line.astype(bf16), (PIECE, det)) > 0.5)
     for i in range(CHUNKS):
         at = slice(i * chunk, (i + 1) * chunk)
-        flat_ref[at, :] = rays_ref[at].reshape(chunk, refl * det)
+        for j in range(i * chunk, (i + 1) * chunk, PIECE):
+            flat = rays_ref[j : j + PIECE].reshape(PIECE, refl * det)
+            for p, keeps in enumerate(stay):
+                first = flat[:, 2 * p * det : (2 * p + 1) * det]
+                second = flat[:, (2 * p + 1) * det : (2 * p + 2) * det]
+                straight = jnp.where(low_block, first, second)
+                crossed = jnp.where(low_block, second, first)
+                flat_ref[j : j + PIECE, p * det : (p + 1) * det] = jnp.where(
+                    keeps, straight, pltpu.roll(crossed, det // 2, 1)
+                )
         if i == 0:
             copy.wait()
         part = jnp.dot(vol_ref[:, at], flat_ref[at, :], preferred_element_type=f32)
         acc[...] = part if i == 0 else acc[...] + part
-    for k in range(refl):
-        proj_ref[k] = acc[:, k * det : (k + 1) * det] * table_ref[MASK + k : MASK + k + 1, :]
+    for k in range(0, refl, 2):
+        both = acc[:, k // 2 * det : (k // 2 + 1) * det]
+        swapped = pltpu.roll(both, det // 2, 1)
+        proj_ref[k] = jnp.where(low, both, swapped) * table_ref[MASK + k : MASK + k + 1, :]
+        proj_ref[k + 1] = jnp.where(low, swapped, both) * table_ref[MASK + k + 1 : MASK + k + 2, :]
 
 
 def project(vol, near, far, rays, table):
@@ -179,10 +198,10 @@
         out_specs=(VMEM, VMEM, VMEM),
         out_shape=(
             jax.ShapeDtypeStruct((refl, ext, det), f32),
-            pltpu.VMEM((cells, refl * det), bf16),
+            pltpu.VMEM((cells, refl * det // 2), bf16),
             pltpu.VMEM((ext, cells), bf16),
         ),
-        scratch_shapes=[pltpu.VMEM((ext, refl * det), f32), pltpu.SemaphoreType.DMA],
+        scratch_shapes=[pltpu.VMEM((ext, refl * det // 2), f32), pltpu.SemaphoreType.DMA],
         compiler_params=pltpu.CompilerParams(vmem_limit_bytes=8 << 20),
         name="project",
     )(keep(vol), near, far, rays, table)
@@ -281,9 +300,15 @@
     steps = cells // chunk
     sends = osem.shape[0]
 
-    img = jnp.concatenate(
-        [img_ref[k] * table_ref[MASK + k : MASK + k + 1, :].astype(bf16) for k in range(refl)], axis=1
-    )
+    low = lax.broadcasted_iota(jnp.int32, (1, det), 1) < det // 2
+    parts = []
+    for k in range(0, refl, 2):
+        first = img_ref[k].astype(f32) * table_ref[MASK + k : MASK + k + 1, :]
+        second = img_ref[k + 1].astype(f32) * table_ref[MASK + k + 1 : MASK + k + 2, :]
+        straight = jnp.where(low, first, second)
+        crossed = jnp.where(low, second, first)
+        parts.append((straight + pltpu.roll(crossed, det // 2, 1)).astype(bf16))
+    img = jnp.concatenate(parts, axis=1)
     scale = table_ref[SCALE : SCALE + 1, 0:1]
 
     place = lax.broadcasted_iota(jnp.int32, (ext, det), 0)

time: 60.9 us -> 58.4 us (0.959)
  Pallas kernels: 18.9 us -> 16.4 us
    pallas_call x1, Pallas kernels: 8.78 us -> 4.96 us  [update(): pl.pallas_call(update_kernel, in_specs=[VMEM] * 4, out_specs=HBM, out_sha...]
    pallas_call x1, Pallas kernels: 7.66 us -> 8.98 us  [project(): pl.pallas_call(project_kernel, in_specs=[HBM, VMEM, VMEM, VMEM, VMEM], ou...]
  transfers between devices with their start and end apart: 8 -> 8, of which waited for: 1 -> 1; matrix products, arithmetic and copies ran while one was open for 0% -> 0% of each run, Pallas kernels for 27% -> 24%
where the time goes in v6:
time: 58.4 us; the launch traced here: 58.1 us
  blocking collectives  28 us (48%)
  Pallas kernels  16.4 us (28%)
  starting transfers between devices  8.56 us (15%)
  waiting for transfers between devices  3.61 us (6%)
  between operations  1.42 us (2%)
    all_to_all x1, blocking collectives, local(): lax.all_to_all(part, 'orient', 0, 0, axis_index_groups=classes, tiled=True)  16.5 us
    all_to_all x1, blocking collectives, local(): lax.all_to_all(total(pieces), 'orient', 0, 0, axis_index_groups=classes,...  11.5 us
    pallas_call x1, Pallas kernels, project(): pl.pallas_call(project_kernel, in_specs=[HBM, VMEM, VMEM, VMEM, VMEM], ou...  8.98 us
    pallas_call x1, Pallas kernels, update(): pl.pallas_call(update_kernel, in_specs=[VMEM] * 4, out_specs=HBM, out_sha...  4.96 us
    ppermute x1, waiting for transfers between devices, local(): far = lax.ppermute(far, 'slab', [(i, slabs - 1 - i) for i in range(slabs)])  3.59 us
    ppermute x3, starting transfers between devices, local(): lax.ppermute(picked[s], 'orient', swaps[s])  3.57 us
    ppermute x3, starting transfers between devices, local(): lax.ppermute(meas_ext, 'orient', swaps[s])  3.57 us
    pallas_call x1, Pallas kernels, prepare(): pl.pallas_call(lambda *refs: prepare_kernel(step_gain, slabs, *refs), in_...  1.37 us
  transfers between devices with their start and end apart: 8, of which 1 were waited for; matrix products, arithmetic and copies ran while one was open for 0% of the time, Pallas kernels for 24%

profile of v6, /device:TPU:24, one launch (start us, length us, event | category | flops | bytes accessed | tf_op | source)
XLA Modules:
  0.0 58.1 jit_solution(13135740996747772409)
XLA Ops:
  1.3 0.0 slice-start
  1.3 0.0 slice-start.1
  1.3 0.0 slice-start.2
  1.3 0.0 slice-start.3
  1.3 1.4 %prepare.1 = (bf16[2,8320]{1,0:T(2,128)(2,1)S(1)}, bf16[2,8320]{1,0:T(2,128)(2,1)S(1)}, f32[128,128]{1,0:T(8,128)S(1)}, f32[80,128]{1,0:T(8,128)S(1)}) custom-call(bf16[128,8192]{1,0:T(8,128)(2,1)} %bitcast.8, f32[128,128]{1,0:T(8,128)} %bitcast.12, s32[8]{0:T(128)} %bitcast.13, s32[8]{0:T(128)} %bitcast.14, s32[32]{0:T(128)} %refs_4_.1, f32[1]{0:T(128)S(6)} %copy.9.refs_5_), custom_call_target="tpu_custom_call" | custom-call | flops 42949672960 | bytes 1048576 | tf_op jit(solution)/shard_map/prepare/pallas_call | solution.py:106
  2.7 0.1 collective-permute-start
  2.8 1.3 %collective-permute-start.1 = (bf16[2,8320]{1,0:T(2,128)(2,1)S(1)}, bf16[2,8320]{1,0:T(2,128)(2,1)S(1)}, u32[]{:S(2)}, u32[]{:S(2)}) collective-permute-start(bf16[2,8320]{1,0:T(2,128)(2,1)S(1)} %get-tuple-element.14), channel_id=1, source_target_pairs={{0,3},{1,2},{2,1},{3,0},{4,7},{5,6},{6,5},{7,4},{8,11},{9,10},{10,... | collective-permute-start | bytes 99848 | tf_op jit(solution)/shard_map/ppermute | solution.py:402
  4.1 0.0 collective-permute-done.near_ref
  4.1 3.6 %collective-permute-done.1.far_ref = bf16[2,8320]{1,0:T(2,128)(2,1)S(1)} collective-permute-done((bf16[2,8320]{1,0:T(2,128)(2,1)S(1)}, bf16[2,8320]{1,0:T(2,128)(2,1)S(1)}, u32[]{:S(2)}, u32[]{:S(2)}) %collective-permute-start.1) | collective-permute-done | bytes 33312 | tf_op jit(solution)/shard_map/ppermute | solution.py:402
  7.7 2.2 %collective-permute-start.4 = (bf16[144,128]{1,0:T(8,128)(2,1)S(1)}, bf16[144,128]{1,0:T(8,128)(2,1)S(1)}, u32[]{:S(2)}, u32[]{:S(2)}) collective-permute-start(bf16[144,128]{1,0:T(8,128)(2,1)S(1)} %extend.1.refs_0_), channel_id=1, source_target_pairs={{0,12},{4,8},{8,4},{12,0},{16,28},{20,24},{24,20},{28,16},{32,44},... | collective-permute-start | bytes 110600 | tf_op jit(solution)/shard_map/ppermute | solution.py:406
  9.9 0.1 collective-permute-start.3
  10.0 1.3 %collective-permute-start.2 = (bf16[144,128]{1,0:T(8,128)(2,1)S(1)}, bf16[144,128]{1,0:T(8,128)(2,1)S(1)}, u32[]{:S(2)}, u32[]{:S(2)}) collective-permute-start(bf16[144,128]{1,0:T(8,128)(2,1)S(1)} %extend.1.refs_0_), channel_id=1, source_target_pairs={{0,4},{4,0},{8,12},{12,8},{16,20},{20,16},{24,28},{28,24},{32,36},... | collective-permute-start | bytes 110600 | tf_op jit(solution)/shard_map/ppermute | solution.py:406
  11.3 0.0 slice-done
  11.3 0.0 slice-done.1
  11.3 0.0 slice-done.2
  11.3 0.0 slice-done.3
  11.3 9.0 %project.1 = (f32[8,144,128]{2,1,0:T(8,128)S(1)}, bf16[8192,512]{1,0:T(8,128)(2,1)S(1)}, bf16[144,8192]{1,0:T(8,128)(2,1)S(1)}) custom-call(bf16[128,8192]{1,0:T(8,128)(2,1)} %bitcast.9, bf16[2,8320]{1,0:T(2,128)(2,1)S(1)} %collective-permute-done.near_ref, bf16[2,8320]{1,0:T(2,128)(2,1)S(1)} %collective-permute-done.1.far_ref, ...), custom_call_target="tpu_custom_call" | custom-call | tf_op jit(solution)/shard_map/project/pallas_call | solution.py:195
  20.3 0.0 collective-permute-done.4.refs_3_
  20.3 0.0 collective-permute-done.3.refs_2_
  20.3 0.0 collective-permute-done.2.refs_1_
  20.4 0.2 combine.1
  20.5 16.5 %all_to_all.10.pieces_ref = bf16[8,144,128]{2,1,0:T(8,128)(2,1)S(1)} all-to-all(bf16[8,144,128]{2,1,0:T(8,128)(2,1)S(1)} %combine.1), channel_id=1, replica_groups={{0,16,32,48,64,80,96,112},{4,20,36,52,68,84,100,116},{8,24,40,56,72,88,..., dimensions={0} | all-to-all | bytes 589824 | tf_op jit(solution)/shard_map/all_to_all | solution.py:411
  37.1 11.5 %all_to_all.11.img_ref = bf16[8,144,128]{2,1,0:T(8,128)(2,1)S(1)} all-to-all(bf16[8,144,128]{2,1,0:T(8,128)(2,1)S(1)} %total.1), channel_id=1, replica_groups={{0,16,32,48,64,80,96,112},{4,20,36,52,68,84,100,116},{8,24,40,56,72,88,..., dimensions={0} | all-to-all | bytes 589824 | tf_op jit(solution)/shard_map/all_to_all | solution.py:412
  48.6 0.2 pick.1
  48.8 0.8 %collective-permute-start.5 = (bf16[128,128]{1,0:T(8,128)(2,1)S(1)}, bf16[128,128]{1,0:T(8,128)(2,1)S(1)}, u32[]{:S(2)}, u32[]{:S(2)}) collective-permute-start(bf16[128,128]{1,0:T(8,128)(2,1)S(1)} %get-tuple-element.21), channel_id=1, source_target_pairs={{0,4},{4,0},{8,12},{12,8},{16,20},{20,16},{24,28},{28,24},{32,36},... | collective-permute-start | bytes 98312 | tf_op jit(solution)/shard_map/ppermute | solution.py:415
  49.6 1.0 %collective-permute-start.6 = (bf16[128,128]{1,0:T(8,128)(2,1)S(1)}, bf16[128,128]{1,0:T(8,128)(2,1)S(1)}, u32[]{:S(2)}, u32[]{:S(2)}) collective-permute-start(bf16[128,128]{1,0:T(8,128)(2,1)S(1)} %get-tuple-element.22), channel_id=1, source_target_pairs={{0,8},{4,12},{8,0},{12,4},{16,24},{20,28},{24,16},{28,20},{32,40},... | collective-permute-start | bytes 98312 | tf_op jit(solution)/shard_map/ppermute | solution.py:415
  50.7 1.7 %collective-permute-start.7 = (bf16[128,128]{1,0:T(8,128)(2,1)S(1)}, bf16[128,128]{1,0:T(8,128)(2,1)S(1)}, u32[]{:S(2)}, u32[]{:S(2)}) collective-permute-start(bf16[128,128]{1,0:T(8,128)(2,1)S(1)} %get-tuple-element.23), channel_id=1, source_target_pairs={{0,12},{4,8},{8,4},{12,0},{16,28},{20,24},{24,20},{28,16},{32,44},... | collective-permute-start | bytes 98312 | tf_op jit(solution)/shard_map/ppermute | solution.py:415
  52.4 5.0 %update.1 = bf16[128,8192]{1,0:T(8,128)(2,1)} custom-call(bf16[8,144,128]{2,1,0:T(8,128)(2,1)S(1)} %all_to_all.11.img_ref, f32[80,128]{1,0:T(8,128)S(1)} %get-tuple-element.15.table_ref, bf16[8192,512]{1,0:T(8,128)(2,1)S(1)} %get-tuple-element.18.flat_ref, bf16[144,8192]{1,0:T(8,128)(2,1)S(1)} %get-tuple-element.19.vol_ref), custom_call_target="tpu_custom_call" | custom-call | tf_op jit(solution)/shard_map/update/pallas_call | solution.py:375
  57.4 0.0 collective-permute-done.5.refs_1_
  57.4 0.0 collective-permute-done.6.refs_2_
  57.4 0.0 collective-permute-done.7.refs_3_
  57.4 0.7 %choose.1 = f32[128,128]{1,0:T(8,128)} custom-call(f32[80,128]{1,0:T(8,128)S(1)} %get-tuple-element.15.table_ref, bf16[128,128]{1,0:T(8,128)(2,1)S(1)} %get-tuple-element.20.refs_0_, bf16[128,128]{1,0:T(8,128)(2,1)S(1)} %collective-permute-done.5.refs_1_, bf16[128,128]{1,0:T(8,128)(2,1)S(1)} %collective-permute-done.6.refs_2_, ...), custom_call_target="tpu_custom_call" | custom-call | tf_op jit(solution)/shard_map/choose/pallas_call | solution.py:283
  (3 shorter events, 0.1 us)
Async XLA Ops:
  1.3 10.0 %slice-start = ((s8[16777216]{0:T(1024)(128)(4,1)}), s8[4194304]{0:T(1024)(128)(4,1)S(1)}, s32[]{:S(2)}) async-start(s8[16777216]{0:T(1024)(128)(4,1)} %bitcast.6), calls=%async_computation.2 | async-start | bytes 8388608
  1.3 10.0 %slice-start.1 = ((s8[16777216]{0:T(1024)(128)(4,1)}), s8[4194304]{0:T(1024)(128)(4,1)S(1)}, s32[]{:S(2)}) async-start(s8[16777216]{0:T(1024)(128)(4,1)} %bitcast.6), calls=%async_computation.3 | async-start | bytes 8388608
  1.3 10.0 %slice-start.2 = ((s8[16777216]{0:T(1024)(128)(4,1)}), s8[4194304]{0:T(1024)(128)(4,1)S(1)}, s32[]{:S(2)}) async-start(s8[16777216]{0:T(1024)(128)(4,1)} %bitcast.6), calls=%async_computation.4 | async-start | bytes 8388608
  1.3 10.0 %slice-start.3 = ((s8[16777216]{0:T(1024)(128)(4,1)}), s8[4194304]{0:T(1024)(128)(4,1)S(1)}, s32[]{:S(2)}) async-start(s8[16777216]{0:T(1024)(128)(4,1)} %bitcast.6), calls=%async_computation.5 | async-start | bytes 8388608
  2.7 1.4 %collective-permute-start = (bf16[2,8320]{1,0:T(2,128)(2,1)S(1)}, bf16[2,8320]{1,0:T(2,128)(2,1)S(1)}, u32[]{:S(2)}, u32[]{:S(2)}) collective-permute-start(bf16[2,8320]{1,0:T(2,128)(2,1)S(1)} %get-tuple-element.13), channel_id=1, source_target_pairs={{0,1},{1,0},{2,3},{3,2},{4,5},{5,4},{6,7},{7,6},{8,9},{9,8},{10,11... | collective-permute-start | bytes 99848 | tf_op jit(solution)/shard_map/ppermute | solution.py:401
  2.8 4.9 %collective-permute-start.1 = (bf16[2,8320]{1,0:T(2,128)(2,1)S(1)}, bf16[2,8320]{1,0:T(2,128)(2,1)S(1)}, u32[]{:S(2)}, u32[]{:S(2)}) collective-permute-start(bf16[2,8320]{1,0:T(2,128)(2,1)S(1)} %get-tuple-element.14), channel_id=1, source_target_pairs={{0,3},{1,2},{2,1},{3,0},{4,7},{5,6},{6,5},{7,4},{8,11},{9,10},{10,... | collective-permute-start | bytes 99848 | tf_op jit(solution)/shard_map/ppermute | solution.py:402
  7.7 12.6 %collective-permute-start.4 = (bf16[144,128]{1,0:T(8,128)(2,1)S(1)}, bf16[144,128]{1,0:T(8,128)(2,1)S(1)}, u32[]{:S(2)}, u32[]{:S(2)}) collective-permute-start(bf16[144,128]{1,0:T(8,128)(2,1)S(1)} %extend.1.refs_0_), channel_id=1, source_target_pairs={{0,12},{4,8},{8,4},{12,0},{16,28},{20,24},{24,20},{28,16},{32,44},... | collective-permute-start | bytes 110600 | tf_op jit(solution)/shard_map/ppermute | solution.py:406
  9.9 10.4 %collective-permute-start.3 = (bf16[144,128]{1,0:T(8,128)(2,1)S(1)}, bf16[144,128]{1,0:T(8,128)(2,1)S(1)}, u32[]{:S(2)}, u32[]{:S(2)}) collective-permute-start(bf16[144,128]{1,0:T(8,128)(2,1)S(1)} %extend.1.refs_0_), channel_id=1, source_target_pairs={{0,8},{4,12},{8,0},{12,4},{16,24},{20,28},{24,16},{28,20},{32,40},... | collective-permute-start | bytes 110600 | tf_op jit(solution)/shard_map/ppermute | solution.py:406
  10.0 10.3 %collective-permute-start.2 = (bf16[144,128]{1,0:T(8,128)(2,1)S(1)}, bf16[144,128]{1,0:T(8,128)(2,1)S(1)}, u32[]{:S(2)}, u32[]{:S(2)}) collective-permute-start(bf16[144,128]{1,0:T(8,128)(2,1)S(1)} %extend.1.refs_0_), channel_id=1, source_target_pairs={{0,4},{4,0},{8,12},{12,8},{16,20},{20,16},{24,28},{28,24},{32,36},... | collective-permute-start | bytes 110600 | tf_op jit(solution)/shard_map/ppermute | solution.py:406
  48.8 8.5 %collective-permute-start.5 = (bf16[128,128]{1,0:T(8,128)(2,1)S(1)}, bf16[128,128]{1,0:T(8,128)(2,1)S(1)}, u32[]{:S(2)}, u32[]{:S(2)}) collective-permute-start(bf16[128,128]{1,0:T(8,128)(2,1)S(1)} %get-tuple-element.21), channel_id=1, source_target_pairs={{0,4},{4,0},{8,12},{12,8},{16,20},{20,16},{24,28},{28,24},{32,36},... | collective-permute-start | bytes 98312 | tf_op jit(solution)/shard_map/ppermute | solution.py:415
  49.6 7.7 %collective-permute-start.6 = (bf16[128,128]{1,0:T(8,128)(2,1)S(1)}, bf16[128,128]{1,0:T(8,128)(2,1)S(1)}, u32[]{:S(2)}, u32[]{:S(2)}) collective-permute-start(bf16[128,128]{1,0:T(8,128)(2,1)S(1)} %get-tuple-element.22), channel_id=1, source_target_pairs={{0,8},{4,12},{8,0},{12,4},{16,24},{20,28},{24,16},{28,20},{32,40},... | collective-permute-start | bytes 98312 | tf_op jit(solution)/shard_map/ppermute | solution.py:415
  50.7 6.7 %collective-permute-start.7 = (bf16[128,128]{1,0:T(8,128)(2,1)S(1)}, bf16[128,128]{1,0:T(8,128)(2,1)S(1)}, u32[]{:S(2)}, u32[]{:S(2)}) collective-permute-start(bf16[128,128]{1,0:T(8,128)(2,1)S(1)} %get-tuple-element.23), channel_id=1, source_target_pairs={{0,12},{4,8},{8,4},{12,0},{16,28},{20,24},{24,20},{28,16},{32,44},... | collective-permute-start | bytes 98312 | tf_op jit(solution)/shard_map/ppermute | solution.py:415
